TPU v7x, 128 devices: a whole 4x4x4 slice. The times are simulated.
128 devices in a mesh: seq: 4 (over y), grp: 32 (over x, z, core).
Axes of the slice: x: 4, y: 4, z: 4, core: 2. Of those that a mesh axis runs over, the one named last changes fastest.
Arguments:
- basis: bfloat16 [128, 2, 32, 1024], replicated, may hold values from -0.109375 to 0.109375
- background: float32 [32, 4, 2, 2, 32, 1024], P('grp', 'seq'), may hold values from -1.2 to 1.2
- detuning: float32 [32], replicated, may hold values from 1 to 4
- dispersion: float32 [32], replicated, may hold values from 0.5 to 2
- neighbors: int32 [32, 2], replicated, may hold values from 0 to 31, as said below
- step_counts: int32 [32, 4], P('grp', 'seq'), may hold values from 1 to 2
Outputs:
- prefix: float32 [32, 4, 128, 128], P('grp', 'seq')
- monodromy: float32 [128, 128], replicated
Inputs may be any that keep to these rules, and one draw needn't show every extreme that they name: `neighbors`: entry (r, k) is cycle r + d or cycle r - d counted around the closed array of 32 cycles, with 1 <= d <= 3; a cycle may be listed twice in one row.
All inputs are finite; a program needn't handle non-finite values.
Results may differ from a plain program's by a relative error of at most 0.0008.
The roundings to bfloat16 on the way count: a program that leaves them out, or rounds other values in their place, can miss the bound.
Values sent between devices are 32-bit elements; how exact they have to be, the bound alone decides.
A program may use at most 192 MiB of HBM per device.

v0:
```python
import math

import jax
import jax.numpy as jnp
from jax import lax
from jax.sharding import PartitionSpec as P

step_size = 0.1
coupling_rate = 1.0
generator_scale = 0.25


def shifted_2(value, axis, steps):
    count = lax.axis_size(axis)
    first, last = (max(0, -steps), min(count, count - steps))
    return lax.ppermute(value, axis, [(source, source + steps) for source in range(first, last)])


def broadcast(x, axis, root):
    mine = lax.axis_index(axis) == root
    return lax.psum(jnp.where(mine, x, jnp.zeros_like(x)), axis)


def coupling_table(neighbors, cycle_count):
    targets = jnp.arange(cycle_count, dtype=jnp.int32)
    matches = (neighbors[:, :, None] == targets[None, None, :]).astype(jnp.float32)
    return jnp.sum(matches, axis=1)


def propagate(vectors, seg_background, step_total, detuning, dispersion, coupling):
    field_state = vectors
    detune_col = detuning[:, None]
    disp_col = dispersion[:, None]
    for step_index in range(seg_background.shape[0]):
        real_bg = seg_background[step_index, 0]
        imag_bg = seg_background[step_index, 1]
        intensity = 2.0 * (real_bg * real_bg + imag_bg * imag_bg)
        square_re = real_bg * real_bg - imag_bg * imag_bg
        square_im = 2.0 * real_bg * imag_bg
        real_part = field_state[:, 0]
        imag_part = field_state[:, 1]
        lap_re = (
            jnp.roll(real_part, 1, axis=-1) + jnp.roll(real_part, -1, axis=-1) - 2.0 * real_part
        )
        lap_im = (
            jnp.roll(imag_part, 1, axis=-1) + jnp.roll(imag_part, -1, axis=-1) - 2.0 * imag_part
        )
        coupled = jnp.einsum(
            "rm,bcmn->bcrn", coupling, field_state, precision=lax.Precision.HIGHEST
        )
        real_rate = (
            -real_part
            + detune_col * imag_part
            - disp_col * lap_im
            - intensity * imag_part
            - square_im * real_part
            + square_re * imag_part
            - coupling_rate * coupled[:, 1]
        )
        imag_rate = (
            -imag_part
            - detune_col * real_part
            + disp_col * lap_re
            + intensity * real_part
            + square_re * real_part
            + square_im * imag_part
            + coupling_rate * coupled[:, 0]
        )
        advanced = field_state + step_size * jnp.stack([real_rate, imag_rate], axis=1)
        field_state = jnp.where(step_index < step_total, advanced, field_state)
    return field_state


def compose(latter, former):
    return jnp.dot(latter, former, precision=lax.Precision.HIGHEST)


def batch_compose(former, latter):
    return jnp.einsum("bij,bjk->bik", latter, former, precision=lax.Precision.HIGHEST)


def cayley(projected):
    generator = generator_scale * (projected - projected.T)
    identity = jnp.eye(projected.shape[0], dtype=jnp.float32)
    plus_gen = identity + generator
    squared = jnp.dot(plus_gen, plus_gen, precision=lax.Precision.HIGHEST)
    normal = identity + jnp.dot(generator.T, generator, precision=lax.Precision.HIGHEST)
    factor = jnp.linalg.cholesky(normal)
    return jax.scipy.linalg.cho_solve((factor, True), squared)


def shards(basis, background, detuning, dispersion, neighbors, step_counts):
    vec_count = basis.shape[0]
    cycle_count = basis.shape[2]
    sample_count = basis.shape[3]
    coupling = coupling_table(neighbors, cycle_count)
    seg_background = background[0, 0]
    step_total = step_counts[0, 0]
    block_width = math.gcd(vec_count, 32)
    vec_blocks = basis.reshape(vec_count // block_width, block_width, 2, cycle_count, sample_count)
    flat_basis = basis.reshape(vec_count, 2 * cycle_count * sample_count)

    def one_block(vec_block):
        field_state = propagate(
            vec_block.astype(jnp.float32),
            seg_background,
            step_total,
            detuning,
            dispersion,
            coupling,
        )
        propagated = field_state.astype(jnp.bfloat16).reshape(
            block_width, 2 * cycle_count * sample_count
        )
        return lax.dot_general(
            flat_basis, propagated, (((1,), (1,)), ((), ())), preferred_element_type=jnp.float32
        )

    columns = lax.map(one_block, vec_blocks)
    projected = jnp.transpose(columns, (1, 0, 2)).reshape(vec_count, vec_count)
    transfer = cayley(projected)
    identity = jnp.eye(vec_count, dtype=jnp.float32)
    seq_count = lax.axis_size("seq")
    seq_pos = lax.axis_index("seq")
    before = identity
    through = transfer
    for hop_index in range(1, seq_count):
        arrived = shifted_2(through, "seq", 1)
        is_mine = seq_pos == hop_index
        before = jnp.where(is_mine, arrived, before)
        through = jnp.where(is_mine, compose(transfer, arrived), through)
    group_product = broadcast(through, "seq", seq_count - 1)
    grp_count = lax.axis_size("grp")
    grp_pos = lax.axis_index("grp")
    totals = lax.all_gather(group_product[None], "grp", axis=0, tiled=True)
    running = lax.associative_scan(batch_compose, totals)
    monodromy = running[grp_count - 1]
    shifted = jnp.concatenate([identity[None], running[:-1]], axis=0)
    earlier = lax.dynamic_index_in_dim(shifted, grp_pos, 0, keepdims=False)
    prefix = compose(before, earlier)
    return (prefix[None, None], monodromy)


def solution(mesh):
    in_specs = (P(), P("grp", "seq", None, None, None, None), P(), P(), P(), P("grp", "seq"))
    out_specs = (P("grp", "seq", None, None), P())
    return jax.shard_map(shards, mesh=mesh, in_specs=in_specs, out_specs=out_specs, check_vma=False)
```

profile of v0, /device:TPU:1, one launch (start us, length us, event | category | flops | bytes accessed | tf_op | source)
XLA Modules:
  0.0 724.8 jit_solution(4332173955934749635)
XLA Ops:
  9.8 18.7 %copy.70 = bf16[16,8,64,1024]{3,1,2,0:T(8,128)(2,1)} copy(bf16[16,8,64,1024]{3,2,1,0:T(8,128)(2,1)} %bitcast.225) | data formatting | bytes 33554432
  28.6 521.6 %while.13 = (s32[]{:T(128)}, f32[4,128,32]{1,2,0:T(8,128)S(1)}, pred[]{:T(512)}, pred[]{:T(512)}, bf16[4,32,2,32,1024]{4,3,2,1,0:T(8,128)(2,1)}, /*index=5*/f32[...) while((s32[]{:T(128)}, f32[4,128,32]{1,2,0:T(8,128)S(1)}, ...), condition=%wide.region_2.3_spmd, body=%wide.region_1.2_spmd.sunk | while | flops 2248343552 | bytes 402679104 | solution.py:119
  29.0 6.8 dynamic-slice_convert_fusion.2
  37.9 7.1 slice_bitcast_fusion.33
  45.0 11.0 %fusion.128 = f32[32,2,32,1024]{3,2,1,0:T(8,128)} fusion(bf16[4,32,2,32,1024]{4,3,2,1,0:T(8,128)(2,1)} %get-tuple-element.440, s32[]{:T(128)} %get-tuple-element.421, f32[32,32]{1,0:T(8,128)S(1)} %get-tuple-element.446), kind=kOutput, calls=%fused_computation.58.clone.1 | convolution fusion | flops 805306368 | bytes 12587520 | tf_op jit(solution)/shard_map/while/body/eval_jaxpr/rm,bcmn->bcrn/dot_general | solution.py:48
  56.7 13.0 %slice_subtract_fusion.4 = (f32[32,1,32,1024]{3,2,1,0:T(8,128)}, f32[32,1,32,1024]{3,2,1,0:T(8,128)}) fusion(f32[32,2,32,1024]{3,2,1,0:T(8,128)} %fusion.128, f32[32,1,32,1023]{3,2,1,0:T(8,128)} %get-tuple-element.377, f32[32,1,32,1]{3,2,1,0:T(8,128)S(1)} %get-tuple-element.378, f32[32,1,32,1]{3,2,1,0:T(8,128)S(1)} %get-tuple-element.379, ...), kind=kLoop, calls=%fused_computation.16.clone.1 | loop fusion | flops 35651584 | bytes 42336512 | tf_op jit(solution)/shard_map/while/body/eval_jaxpr/sub | solution.py:52
  69.7 8.1 %maximum_multiply_fusion.4 = (f32[32,2,32,1024]{3,2,1,0:T(8,128)}, f32[32,2,32,1024]{3,2,1,0:T(8,128)S(1)}) fusion(f32[32,1,32,1024]{3,2,1,0:T(8,128)} %get-tuple-element.387, f32[32,1,32,1024]{3,2,1,0:T(8,128)} %get-tuple-element.388, bf16[4,32,2,32,1024]{4,3,2,1,0:T(8,128)(2,1)} %get-tuple-element.440, s32[]{:T(128)} %get-tuple-element.421, ...), kind=kLoop, calls=%fused_computation.4.clone.2 | loop fusion | flops 10485760 | bytes 29360132 | tf_op jit(solution)/shard_map/while/body/eval_jaxpr/mul | solution.py:69
  89.2 10.6 %convolution_bitcast_fusion.5 = f32[32,2,32,1024]{3,2,1,0:T(8,128)} fusion(f32[32,2,32,1024]{3,2,1,0:T(8,128)S(1)} %get-tuple-element.389, f32[32,32]{1,0:T(8,128)S(1)} %get-tuple-element.446), kind=kOutput, calls=%fused_computation.57.clone.1 | convolution fusion | flops 805306368 | bytes 16781312 | tf_op jit(solution)/shard_map/while/body/eval_jaxpr/rm,bcmn->bcrn/dot_general | solution.py:48
  99.8 13.1 %slice_subtract_fusion.5 = (f32[32,1,32,1024]{3,2,1,0:T(8,128)}, f32[32,1,32,1024]{3,2,1,0:T(8,128)}) fusion(f32[32,2,32,1024]{3,2,1,0:T(8,128)} %convolution_bitcast_fusion.5, f32[32,1,32,1023]{3,2,1,0:T(8,128)} %get-tuple-element.391, f32[32,1,32,1]{3,2,1,0:T(8,128)S(1)} %get-tuple-element.392, f32[32,1,32,1]{3,2,1,0:T(8,128)S(1)} %get-tuple-element.393, ...), kind=kLoop, calls=%fused_computation.10.clone.1 | loop fusion | flops 35651584 | bytes 42336512 | tf_op jit(solution)/shard_map/while/body/eval_jaxpr/sub | solution.py:52
  117.5 8.1 %copy.73 = f32[4,8,64,1024]{3,1,2,0:T(8,128)} copy(f32[4,8,64,1024]{3,2,1,0:T(8,128)S(1)} %bitcast.221) | data formatting | bytes 16777216 | tf_op jit(solution)/shard_map/while
  125.6 8.1 %copy.74 = f32[4,8,64,1024]{3,1,2,0:T(8,128)} copy(f32[4,8,64,1024]{3,2,1,0:T(8,128)S(1)} %bitcast.220) | data formatting | bytes 16777216 | tf_op jit(solution)/shard_map/while
  133.7 7.5 %reshape.510 = f32[32,65536]{1,0:T(8,128)} reshape(f32[1,32,2,32,1024]{4,3,2,1,0:T(8,128)} %get-tuple-element.404) | data formatting | bytes 16777216 | tf_op jit(solution)/shard_map/while/body/eval_jaxpr/convert_element_type | solution.py:105
  141.1 16.0 %fusion.129 = f32[4,128,32]{1,2,0:T(8,128)S(1)} fusion(f32[4,128,32]{1,2,0:T(8,128)S(1)} %get-tuple-element.422, s32[]{:T(128)} %get-tuple-element.421, bf16[128,65536]{1,0:T(8,128)(2,1)} %get-tuple-element.449, f32[32,65536]{1,0:T(8,128)} %bitcast.222, f32[32,65536]{1,0:T(8,128)} %reshape.510, f32[32,65536]{1,0:T(8,128)} %bitcast.223, ...), kind=kOutput, calls=%fused_computation.62.clone.1 | convolution fusion | flops 547356672 | bytes 41959432 | tf_op jit(solution)/shard_map/while/body/eval_jaxpr/dot_general | solution.py:115
  157.6 6.8 dynamic-slice_convert_fusion.2
  166.5 7.1 slice_bitcast_fusion.33
  173.6 11.0 %fusion.128 = f32[32,2,32,1024]{3,2,1,0:T(8,128)} fusion(bf16[4,32,2,32,1024]{4,3,2,1,0:T(8,128)(2,1)} %get-tuple-element.440, s32[]{:T(128)} %get-tuple-element.421, f32[32,32]{1,0:T(8,128)S(1)} %get-tuple-element.446), kind=kOutput, calls=%fused_computation.58.clone.1 | convolution fusion | flops 805306368 | bytes 12587520 | tf_op jit(solution)/shard_map/while/body/eval_jaxpr/rm,bcmn->bcrn/dot_general | solution.py:48
  185.3 13.0 %slice_subtract_fusion.4 = (f32[32,1,32,1024]{3,2,1,0:T(8,128)}, f32[32,1,32,1024]{3,2,1,0:T(8,128)}) fusion(f32[32,2,32,1024]{3,2,1,0:T(8,128)} %fusion.128, f32[32,1,32,1023]{3,2,1,0:T(8,128)} %get-tuple-element.377, f32[32,1,32,1]{3,2,1,0:T(8,128)S(1)} %get-tuple-element.378, f32[32,1,32,1]{3,2,1,0:T(8,128)S(1)} %get-tuple-element.379, ...), kind=kLoop, calls=%fused_computation.16.clone.1 | loop fusion | flops 35651584 | bytes 42336512 | tf_op jit(solution)/shard_map/while/body/eval_jaxpr/sub | solution.py:52
  198.3 7.9 %maximum_multiply_fusion.4 = (f32[32,2,32,1024]{3,2,1,0:T(8,128)}, f32[32,2,32,1024]{3,2,1,0:T(8,128)S(1)}) fusion(f32[32,1,32,1024]{3,2,1,0:T(8,128)} %get-tuple-element.387, f32[32,1,32,1024]{3,2,1,0:T(8,128)} %get-tuple-element.388, bf16[4,32,2,32,1024]{4,3,2,1,0:T(8,128)(2,1)} %get-tuple-element.440, s32[]{:T(128)} %get-tuple-element.421, ...), kind=kLoop, calls=%fused_computation.4.clone.2 | loop fusion | flops 10485760 | bytes 29360132 | tf_op jit(solution)/shard_map/while/body/eval_jaxpr/mul | solution.py:69
  217.6 10.6 %convolution_bitcast_fusion.5 = f32[32,2,32,1024]{3,2,1,0:T(8,128)} fusion(f32[32,2,32,1024]{3,2,1,0:T(8,128)S(1)} %get-tuple-element.389, f32[32,32]{1,0:T(8,128)S(1)} %get-tuple-element.446), kind=kOutput, calls=%fused_computation.57.clone.1 | convolution fusion | flops 805306368 | bytes 16781312 | tf_op jit(solution)/shard_map/while/body/eval_jaxpr/rm,bcmn->bcrn/dot_general | solution.py:48
  228.2 13.4 %slice_subtract_fusion.5 = (f32[32,1,32,1024]{3,2,1,0:T(8,128)}, f32[32,1,32,1024]{3,2,1,0:T(8,128)}) fusion(f32[32,2,32,1024]{3,2,1,0:T(8,128)} %convolution_bitcast_fusion.5, f32[32,1,32,1023]{3,2,1,0:T(8,128)} %get-tuple-element.391, f32[32,1,32,1]{3,2,1,0:T(8,128)S(1)} %get-tuple-element.392, f32[32,1,32,1]{3,2,1,0:T(8,128)S(1)} %get-tuple-element.393, ...), kind=kLoop, calls=%fused_computation.10.clone.1 | loop fusion | flops 35651584 | bytes 42336512 | tf_op jit(solution)/shard_map/while/body/eval_jaxpr/sub | solution.py:52
  246.1 8.1 %copy.73 = f32[4,8,64,1024]{3,1,2,0:T(8,128)} copy(f32[4,8,64,1024]{3,2,1,0:T(8,128)S(1)} %bitcast.221) | data formatting | bytes 16777216 | tf_op jit(solution)/shard_map/while
  254.2 8.1 %copy.74 = f32[4,8,64,1024]{3,1,2,0:T(8,128)} copy(f32[4,8,64,1024]{3,2,1,0:T(8,128)S(1)} %bitcast.220) | data formatting | bytes 16777216 | tf_op jit(solution)/shard_map/while
  262.3 7.5 %reshape.510 = f32[32,65536]{1,0:T(8,128)} reshape(f32[1,32,2,32,1024]{4,3,2,1,0:T(8,128)} %get-tuple-element.404) | data formatting | bytes 16777216 | tf_op jit(solution)/shard_map/while/body/eval_jaxpr/convert_element_type | solution.py:105
  269.8 16.0 %fusion.129 = f32[4,128,32]{1,2,0:T(8,128)S(1)} fusion(f32[4,128,32]{1,2,0:T(8,128)S(1)} %get-tuple-element.422, s32[]{:T(128)} %get-tuple-element.421, bf16[128,65536]{1,0:T(8,128)(2,1)} %get-tuple-element.449, f32[32,65536]{1,0:T(8,128)} %bitcast.222, f32[32,65536]{1,0:T(8,128)} %reshape.510, f32[32,65536]{1,0:T(8,128)} %bitcast.223, ...), kind=kOutput, calls=%fused_computation.62.clone.1 | convolution fusion | flops 547356672 | bytes 41959432 | tf_op jit(solution)/shard_map/while/body/eval_jaxpr/dot_general | solution.py:115
  294.9 7.1 slice_bitcast_fusion.33
  302.0 11.0 %fusion.128 = f32[32,2,32,1024]{3,2,1,0:T(8,128)} fusion(bf16[4,32,2,32,1024]{4,3,2,1,0:T(8,128)(2,1)} %get-tuple-element.440, s32[]{:T(128)} %get-tuple-element.421, f32[32,32]{1,0:T(8,128)S(1)} %get-tuple-element.446), kind=kOutput, calls=%fused_computation.58.clone.1 | convolution fusion | flops 805306368 | bytes 12587520 | tf_op jit(solution)/shard_map/while/body/eval_jaxpr/rm,bcmn->bcrn/dot_general | solution.py:48
  313.7 13.0 %slice_subtract_fusion.4 = (f32[32,1,32,1024]{3,2,1,0:T(8,128)}, f32[32,1,32,1024]{3,2,1,0:T(8,128)}) fusion(f32[32,2,32,1024]{3,2,1,0:T(8,128)} %fusion.128, f32[32,1,32,1023]{3,2,1,0:T(8,128)} %get-tuple-element.377, f32[32,1,32,1]{3,2,1,0:T(8,128)S(1)} %get-tuple-element.378, f32[32,1,32,1]{3,2,1,0:T(8,128)S(1)} %get-tuple-element.379, ...), kind=kLoop, calls=%fused_computation.16.clone.1 | loop fusion | flops 35651584 | bytes 42336512 | tf_op jit(solution)/shard_map/while/body/eval_jaxpr/sub | solution.py:52
  326.7 8.1 %maximum_multiply_fusion.4 = (f32[32,2,32,1024]{3,2,1,0:T(8,128)}, f32[32,2,32,1024]{3,2,1,0:T(8,128)S(1)}) fusion(f32[32,1,32,1024]{3,2,1,0:T(8,128)} %get-tuple-element.387, f32[32,1,32,1024]{3,2,1,0:T(8,128)} %get-tuple-element.388, bf16[4,32,2,32,1024]{4,3,2,1,0:T(8,128)(2,1)} %get-tuple-element.440, s32[]{:T(128)} %get-tuple-element.421, ...), kind=kLoop, calls=%fused_computation.4.clone.2 | loop fusion | flops 10485760 | bytes 29360132 | tf_op jit(solution)/shard_map/while/body/eval_jaxpr/mul | solution.py:69
  346.3 10.6 %convolution_bitcast_fusion.5 = f32[32,2,32,1024]{3,2,1,0:T(8,128)} fusion(f32[32,2,32,1024]{3,2,1,0:T(8,128)S(1)} %get-tuple-element.389, f32[32,32]{1,0:T(8,128)S(1)} %get-tuple-element.446), kind=kOutput, calls=%fused_computation.57.clone.1 | convolution fusion | flops 805306368 | bytes 16781312 | tf_op jit(solution)/shard_map/while/body/eval_jaxpr/rm,bcmn->bcrn/dot_general | solution.py:48
  356.9 13.1 %slice_subtract_fusion.5 = (f32[32,1,32,1024]{3,2,1,0:T(8,128)}, f32[32,1,32,1024]{3,2,1,0:T(8,128)}) fusion(f32[32,2,32,1024]{3,2,1,0:T(8,128)} %convolution_bitcast_fusion.5, f32[32,1,32,1023]{3,2,1,0:T(8,128)} %get-tuple-element.391, f32[32,1,32,1]{3,2,1,0:T(8,128)S(1)} %get-tuple-element.392, f32[32,1,32,1]{3,2,1,0:T(8,128)S(1)} %get-tuple-element.393, ...), kind=kLoop, calls=%fused_computation.10.clone.1 | loop fusion | flops 35651584 | bytes 42336512 | tf_op jit(solution)/shard_map/while/body/eval_jaxpr/sub | solution.py:52
  374.5 8.1 %copy.73 = f32[4,8,64,1024]{3,1,2,0:T(8,128)} copy(f32[4,8,64,1024]{3,2,1,0:T(8,128)S(1)} %bitcast.221) | data formatting | bytes 16777216 | tf_op jit(solution)/shard_map/while
  382.6 8.1 %copy.74 = f32[4,8,64,1024]{3,1,2,0:T(8,128)} copy(f32[4,8,64,1024]{3,2,1,0:T(8,128)S(1)} %bitcast.220) | data formatting | bytes 16777216 | tf_op jit(solution)/shard_map/while
  390.7 7.5 %reshape.510 = f32[32,65536]{1,0:T(8,128)} reshape(f32[1,32,2,32,1024]{4,3,2,1,0:T(8,128)} %get-tuple-element.404) | data formatting | bytes 16777216 | tf_op jit(solution)/shard_map/while/body/eval_jaxpr/convert_element_type | solution.py:105
  398.2 16.0 %fusion.129 = f32[4,128,32]{1,2,0:T(8,128)S(1)} fusion(f32[4,128,32]{1,2,0:T(8,128)S(1)} %get-tuple-element.422, s32[]{:T(128)} %get-tuple-element.421, bf16[128,65536]{1,0:T(8,128)(2,1)} %get-tuple-element.449, f32[32,65536]{1,0:T(8,128)} %bitcast.222, f32[32,65536]{1,0:T(8,128)} %reshape.510, f32[32,65536]{1,0:T(8,128)} %bitcast.223, ...), kind=kOutput, calls=%fused_computation.62.clone.1 | convolution fusion | flops 547356672 | bytes 41959432 | tf_op jit(solution)/shard_map/while/body/eval_jaxpr/dot_general | solution.py:115
  423.6 7.1 slice_bitcast_fusion.33
  430.7 11.0 %fusion.128 = f32[32,2,32,1024]{3,2,1,0:T(8,128)} fusion(bf16[4,32,2,32,1024]{4,3,2,1,0:T(8,128)(2,1)} %get-tuple-element.440, s32[]{:T(128)} %get-tuple-element.421, f32[32,32]{1,0:T(8,128)S(1)} %get-tuple-element.446), kind=kOutput, calls=%fused_computation.58.clone.1 | convolution fusion | flops 805306368 | bytes 12587520 | tf_op jit(solution)/shard_map/while/body/eval_jaxpr/rm,bcmn->bcrn/dot_general | solution.py:48
  442.3 13.0 %slice_subtract_fusion.4 = (f32[32,1,32,1024]{3,2,1,0:T(8,128)}, f32[32,1,32,1024]{3,2,1,0:T(8,128)}) fusion(f32[32,2,32,1024]{3,2,1,0:T(8,128)} %fusion.128, f32[32,1,32,1023]{3,2,1,0:T(8,128)} %get-tuple-element.377, f32[32,1,32,1]{3,2,1,0:T(8,128)S(1)} %get-tuple-element.378, f32[32,1,32,1]{3,2,1,0:T(8,128)S(1)} %get-tuple-element.379, ...), kind=kLoop, calls=%fused_computation.16.clone.1 | loop fusion | flops 35651584 | bytes 42336512 | tf_op jit(solution)/shard_map/while/body/eval_jaxpr/sub | solution.py:52
  455.4 7.9 %maximum_multiply_fusion.4 = (f32[32,2,32,1024]{3,2,1,0:T(8,128)}, f32[32,2,32,1024]{3,2,1,0:T(8,128)S(1)}) fusion(f32[32,1,32,1024]{3,2,1,0:T(8,128)} %get-tuple-element.387, f32[32,1,32,1024]{3,2,1,0:T(8,128)} %get-tuple-element.388, bf16[4,32,2,32,1024]{4,3,2,1,0:T(8,128)(2,1)} %get-tuple-element.440, s32[]{:T(128)} %get-tuple-element.421, ...), kind=kLoop, calls=%fused_computation.4.clone.2 | loop fusion | flops 10485760 | bytes 29360132 | tf_op jit(solution)/shard_map/while/body/eval_jaxpr/mul | solution.py:69
  474.7 10.6 %convolution_bitcast_fusion.5 = f32[32,2,32,1024]{3,2,1,0:T(8,128)} fusion(f32[32,2,32,1024]{3,2,1,0:T(8,128)S(1)} %get-tuple-element.389, f32[32,32]{1,0:T(8,128)S(1)} %get-tuple-element.446), kind=kOutput, calls=%fused_computation.57.clone.1 | convolution fusion | flops 805306368 | bytes 16781312 | tf_op jit(solution)/shard_map/while/body/eval_jaxpr/rm,bcmn->bcrn/dot_general | solution.py:48
  485.3 13.4 %slice_subtract_fusion.5 = (f32[32,1,32,1024]{3,2,1,0:T(8,128)}, f32[32,1,32,1024]{3,2,1,0:T(8,128)}) fusion(f32[32,2,32,1024]{3,2,1,0:T(8,128)} %convolution_bitcast_fusion.5, f32[32,1,32,1023]{3,2,1,0:T(8,128)} %get-tuple-element.391, f32[32,1,32,1]{3,2,1,0:T(8,128)S(1)} %get-tuple-element.392, f32[32,1,32,1]{3,2,1,0:T(8,128)S(1)} %get-tuple-element.393, ...), kind=kLoop, calls=%fused_computation.10.clone.1 | loop fusion | flops 35651584 | bytes 42336512 | tf_op jit(solution)/shard_map/while/body/eval_jaxpr/sub | solution.py:52
  503.2 8.1 %copy.73 = f32[4,8,64,1024]{3,1,2,0:T(8,128)} copy(f32[4,8,64,1024]{3,2,1,0:T(8,128)S(1)} %bitcast.221) | data formatting | bytes 16777216 | tf_op jit(solution)/shard_map/while
  511.3 8.1 %copy.74 = f32[4,8,64,1024]{3,1,2,0:T(8,128)} copy(f32[4,8,64,1024]{3,2,1,0:T(8,128)S(1)} %bitcast.220) | data formatting | bytes 16777216 | tf_op jit(solution)/shard_map/while
  519.4 7.5 %reshape.510 = f32[32,65536]{1,0:T(8,128)} reshape(f32[1,32,2,32,1024]{4,3,2,1,0:T(8,128)} %get-tuple-element.404) | data formatting | bytes 16777216 | tf_op jit(solution)/shard_map/while/body/eval_jaxpr/convert_element_type | solution.py:105
  526.8 16.0 %fusion.129 = f32[4,128,32]{1,2,0:T(8,128)S(1)} fusion(f32[4,128,32]{1,2,0:T(8,128)S(1)} %get-tuple-element.422, s32[]{:T(128)} %get-tuple-element.421, bf16[128,65536]{1,0:T(8,128)(2,1)} %get-tuple-element.449, f32[32,65536]{1,0:T(8,128)} %bitcast.222, f32[32,65536]{1,0:T(8,128)} %reshape.510, f32[32,65536]{1,0:T(8,128)} %bitcast.223, ...), kind=kOutput, calls=%fused_computation.62.clone.1 | convolution fusion | flops 547356672 | bytes 41959432 | tf_op jit(solution)/shard_map/while/body/eval_jaxpr/dot_general | solution.py:115
  551.0 11.7 %cholesky.19 = f32[128,128]{1,0:T(8,128)S(1)} custom-call(f32[128,128]{1,0:T(8,128)S(1)} %fusion.77), custom_call_target="Cholesky" | custom-call | tf_op jit(solution)/shard_map/jit(cholesky)/cholesky | solution.py:88
  564.0 9.8 %custom-call.10 = f32[1,128,128]{1,2,0:T(8,128)S(1)} custom-call(f32[1,128,128]{2,1,0:T(8,128)S(1)} %fusion.75), custom_call_target="InvertDiagBlocksLowerTriangular" | custom-call | tf_op jit(solution)/shard_map/jit(_cho_solve)/triangular_solve | solution.py:89
  591.1 45.2 %all-reduce.12.cloned.1.call-done = f32[1,128,128]{2,1,0:T(8,128)} async-done(((f32[1,128,128]{2,1,0:T(8,128)}), f32[1,128,128]{2,1,0:T(8,128)}) %all-reduce.12.cloned.1.call-update) | async-done | bytes 65552 | tf_op jit(solution)/shard_map/psum | solution.py:21
  636.3 49.3 %all-gather.2.cloned.1.call-done = f32[32,128,128]{2,1,0:T(8,128)} async-done(((f32[1,128,128]{2,1,0:T(8,128)}), f32[32,128,128]{2,1,0:T(8,128)}) %all-gather.2.cloned.1.call-update) | async-done | bytes 2097168 | tf_op jit(solution)/shard_map/all_gather | solution.py:135
  (165 shorter events, 141.1 us)
Async XLA Ops:
  7.2 629.1 %all-reduce.12.cloned.1.call-start = ((), (), s32[]{:S(2)}) async-start(), calls=%async_computation | async-start | bytes 131072 | tf_op jit(solution)/shard_map/psum | solution.py:21
  9.7 18.8 %copy-start.7 = (s32[32,2]{0,1:T(2,128)S(1)}, s32[32,2]{0,1:T(2,128)}, u32[]{:S(2)}) copy-start(s32[32,2]{0,1:T(2,128)} %param.12) | copy-start | bytes 772
  9.8 18.8 %copy-start = (f32[1,1,2,2,32,1024]{5,4,3,2,1,0:T(8,128)S(1)}, f32[1,1,2,2,32,1024]{5,4,3,2,1,0:T(8,128)}, u32[]{:S(2)}) copy-start(f32[1,1,2,2,32,1024]{5,4,3,2,1,0:T(8,128)} %param.9) | copy-start | bytes 1572868
  9.8 18.8 %copy-start.6 = (f32[32]{0:T(128)S(1)}, f32[32]{0:T(128)}, u32[]{:S(2)}) copy-start(f32[32]{0:T(128)} %param.10) | copy-start | bytes 388
  29.0 27.0 %copy-start.3 = (f32[1,32,1024]{2,1,0:T(8,128)}, f32[1,32,1024]{2,1,0:T(8,128)S(1)}, u32[]{:S(2)}) copy-start(f32[1,32,1024]{2,1,0:T(8,128)S(1)} %get-tuple-element.447) | copy-start | bytes 393220 | tf_op jit(solution)/shard_map/while
  45.0 11.0 %copy-start.5 = (f32[1,32,1024]{2,1,0:T(8,128)S(1)}, f32[1,32,1024]{2,1,0:T(8,128)}, u32[]{:S(2)}) copy-start(f32[1,32,1024]{2,1,0:T(8,128)} %get-tuple-element.443) | copy-start | bytes 393220 | tf_op jit(solution)/shard_map/while
  89.2 10.6 %copy-start.2 = (f32[1,32,1024]{2,1,0:T(8,128)S(1)}, f32[1,32,1024]{2,1,0:T(8,128)}, u32[]{:S(2)}) copy-start(f32[1,32,1024]{2,1,0:T(8,128)} %get-tuple-element.448) | copy-start | bytes 393220 | tf_op jit(solution)/shard_map/while
  117.5 8.1 %slice-start = ((s8[8388608]{0:T(1024)(128)(4,1)}), s8[4194304]{0:T(1024)(128)(4,1)S(1)}, s32[]{:S(2)}) async-start(s8[8388608]{0:T(1024)(128)(4,1)} %bitcast.218), calls=%async_computation.2 | async-start | bytes 8388608 | tf_op jit(solution)/shard_map/while
  117.5 8.1 %slice-start.1 = ((s8[8388608]{0:T(1024)(128)(4,1)}), s8[4194304]{0:T(1024)(128)(4,1)S(1)}, s32[]{:S(2)}) async-start(s8[8388608]{0:T(1024)(128)(4,1)} %bitcast.218), calls=%async_computation.3 | async-start | bytes 8388608 | tf_op jit(solution)/shard_map/while
  141.1 16.0 %copy-start.4 = (f32[1,32,1024]{2,1,0:T(8,128)S(1)}, f32[1,32,1024]{2,1,0:T(8,128)}, u32[]{:S(2)}) copy-start(f32[1,32,1024]{2,1,0:T(8,128)} %copy-done.3) | copy-start | bytes 393220 | tf_op jit(solution)/shard_map/while
  157.6 27.0 %copy-start.3 = (f32[1,32,1024]{2,1,0:T(8,128)}, f32[1,32,1024]{2,1,0:T(8,128)S(1)}, u32[]{:S(2)}) copy-start(f32[1,32,1024]{2,1,0:T(8,128)S(1)} %get-tuple-element.447) | copy-start | bytes 393220 | tf_op jit(solution)/shard_map/while
  173.6 11.0 %copy-start.5 = (f32[1,32,1024]{2,1,0:T(8,128)S(1)}, f32[1,32,1024]{2,1,0:T(8,128)}, u32[]{:S(2)}) copy-start(f32[1,32,1024]{2,1,0:T(8,128)} %get-tuple-element.443) | copy-start | bytes 393220 | tf_op jit(solution)/shard_map/while
  217.6 10.6 %copy-start.2 = (f32[1,32,1024]{2,1,0:T(8,128)S(1)}, f32[1,32,1024]{2,1,0:T(8,128)}, u32[]{:S(2)}) copy-start(f32[1,32,1024]{2,1,0:T(8,128)} %get-tuple-element.448) | copy-start | bytes 393220 | tf_op jit(solution)/shard_map/while
  246.1 8.1 %slice-start = ((s8[8388608]{0:T(1024)(128)(4,1)}), s8[4194304]{0:T(1024)(128)(4,1)S(1)}, s32[]{:S(2)}) async-start(s8[8388608]{0:T(1024)(128)(4,1)} %bitcast.218), calls=%async_computation.2 | async-start | bytes 8388608 | tf_op jit(solution)/shard_map/while
  246.1 8.1 %slice-start.1 = ((s8[8388608]{0:T(1024)(128)(4,1)}), s8[4194304]{0:T(1024)(128)(4,1)S(1)}, s32[]{:S(2)}) async-start(s8[8388608]{0:T(1024)(128)(4,1)} %bitcast.218), calls=%async_computation.3 | async-start | bytes 8388608 | tf_op jit(solution)/shard_map/while
  269.8 16.0 %copy-start.4 = (f32[1,32,1024]{2,1,0:T(8,128)S(1)}, f32[1,32,1024]{2,1,0:T(8,128)}, u32[]{:S(2)}) copy-start(f32[1,32,1024]{2,1,0:T(8,128)} %copy-done.3) | copy-start | bytes 393220 | tf_op jit(solution)/shard_map/while
  286.0 27.0 %copy-start.3 = (f32[1,32,1024]{2,1,0:T(8,128)}, f32[1,32,1024]{2,1,0:T(8,128)S(1)}, u32[]{:S(2)}) copy-start(f32[1,32,1024]{2,1,0:T(8,128)S(1)} %get-tuple-element.447) | copy-start | bytes 393220 | tf_op jit(solution)/shard_map/while
  302.0 11.0 %copy-start.5 = (f32[1,32,1024]{2,1,0:T(8,128)S(1)}, f32[1,32,1024]{2,1,0:T(8,128)}, u32[]{:S(2)}) copy-start(f32[1,32,1024]{2,1,0:T(8,128)} %get-tuple-element.443) | copy-start | bytes 393220 | tf_op jit(solution)/shard_map/while
  346.3 10.6 %copy-start.2 = (f32[1,32,1024]{2,1,0:T(8,128)S(1)}, f32[1,32,1024]{2,1,0:T(8,128)}, u32[]{:S(2)}) copy-start(f32[1,32,1024]{2,1,0:T(8,128)} %get-tuple-element.448) | copy-start | bytes 393220 | tf_op jit(solution)/shard_map/while
  374.5 8.1 %slice-start = ((s8[8388608]{0:T(1024)(128)(4,1)}), s8[4194304]{0:T(1024)(128)(4,1)S(1)}, s32[]{:S(2)}) async-start(s8[8388608]{0:T(1024)(128)(4,1)} %bitcast.218), calls=%async_computation.2 | async-start | bytes 8388608 | tf_op jit(solution)/shard_map/while
  374.5 8.1 %slice-start.1 = ((s8[8388608]{0:T(1024)(128)(4,1)}), s8[4194304]{0:T(1024)(128)(4,1)S(1)}, s32[]{:S(2)}) async-start(s8[8388608]{0:T(1024)(128)(4,1)} %bitcast.218), calls=%async_computation.3 | async-start | bytes 8388608 | tf_op jit(solution)/shard_map/while
  398.2 16.0 %copy-start.4 = (f32[1,32,1024]{2,1,0:T(8,128)S(1)}, f32[1,32,1024]{2,1,0:T(8,128)}, u32[]{:S(2)}) copy-start(f32[1,32,1024]{2,1,0:T(8,128)} %copy-done.3) | copy-start | bytes 393220 | tf_op jit(solution)/shard_map/while
  414.6 27.0 %copy-start.3 = (f32[1,32,1024]{2,1,0:T(8,128)}, f32[1,32,1024]{2,1,0:T(8,128)S(1)}, u32[]{:S(2)}) copy-start(f32[1,32,1024]{2,1,0:T(8,128)S(1)} %get-tuple-element.447) | copy-start | bytes 393220 | tf_op jit(solution)/shard_map/while
  430.7 11.0 %copy-start.5 = (f32[1,32,1024]{2,1,0:T(8,128)S(1)}, f32[1,32,1024]{2,1,0:T(8,128)}, u32[]{:S(2)}) copy-start(f32[1,32,1024]{2,1,0:T(8,128)} %get-tuple-element.443) | copy-start | bytes 393220 | tf_op jit(solution)/shard_map/while
  474.7 10.6 %copy-start.2 = (f32[1,32,1024]{2,1,0:T(8,128)S(1)}, f32[1,32,1024]{2,1,0:T(8,128)}, u32[]{:S(2)}) copy-start(f32[1,32,1024]{2,1,0:T(8,128)} %get-tuple-element.448) | copy-start | bytes 393220 | tf_op jit(solution)/shard_map/while
  503.2 8.1 %slice-start = ((s8[8388608]{0:T(1024)(128)(4,1)}), s8[4194304]{0:T(1024)(128)(4,1)S(1)}, s32[]{:S(2)}) async-start(s8[8388608]{0:T(1024)(128)(4,1)} %bitcast.218), calls=%async_computation.2 | async-start | bytes 8388608 | tf_op jit(solution)/shard_map/while
  503.2 8.1 %slice-start.1 = ((s8[8388608]{0:T(1024)(128)(4,1)}), s8[4194304]{0:T(1024)(128)(4,1)S(1)}, s32[]{:S(2)}) async-start(s8[8388608]{0:T(1024)(128)(4,1)} %bitcast.218), calls=%async_computation.3 | async-start | bytes 8388608 | tf_op jit(solution)/shard_map/while
  526.8 16.0 %copy-start.4 = (f32[1,32,1024]{2,1,0:T(8,128)S(1)}, f32[1,32,1024]{2,1,0:T(8,128)}, u32[]{:S(2)}) copy-start(f32[1,32,1024]{2,1,0:T(8,128)} %copy-done.3) | copy-start | bytes 393220 | tf_op jit(solution)/shard_map/while
  574.4 5.4 collective-permute-start
  579.9 5.0 collective-permute-start.1
  585.1 5.0 collective-permute-start.2
  591.0 94.6 %all-gather.2.cloned.1.call-start = ((), (), s32[]{:S(2)}) async-start(), calls=%async_computation.1 | async-start | bytes 2162688 | tf_op jit(solution)/shard_map/all_gather | solution.py:135
  698.5 8.6 %slice-start.2 = ((f32[32,128,128]{2,1,0:T(8,128)}), f32[1,128,128]{2,1,0:T(8,128)S(1)}, s32[]{:S(2)}) async-start(f32[32,128,128]{2,1,0:T(8,128)} %all-gather.2.cloned.1.call-done), calls=%async_computation.4 | async-start | bytes 131072 | tf_op jit(solution)/shard_map/slice | solution.py:136
  707.1 7.9 %copy-start.1 = (f32[32,128,128]{2,1,0:T(8,128)S(1)}, f32[32,128,128]{2,1,0:T(8,128)}, u32[]{:S(2)}) copy-start(f32[32,128,128]{2,1,0:T(8,128)} %pad.40) | copy-start | bytes 6291460
Sparse Core Ops, SparseCore 0:
  591.1 45.1 all-reduce.11
  638.8 46.7 all-gather.1
where the time goes:
time: 728 us; the launch traced here: 725 us
  local copies, waits for them, and re-layouts  215 us (30%)
  other arithmetic  214 us (29%)
  matrix products  161 us (22%)
  waiting for transfers between devices  98.4 us (14%)
  between operations  15.4 us (2%)
  starting transfers between devices  11.5 us (2%)
  loops' own time  9.17 us (1%)
    sub x8, other arithmetic, propagate(): -real_part + detune_col * imag_part - disp_col * lap_im  105 us
    dot_general x8, matrix products, propagate(): jnp.einsum('rm,bcmn->bcrn', coupling, field_state, precision=lax.Precisio...  86.4 us
    while x56, local copies, waits for them, and re-layouts  64.8 us
    dot_general x4, matrix products, one_block(): lax.dot_general(flat_basis, propagated, (((1,), (1,)), ((), ())), preferr...  64 us
    mul x8, other arithmetic, propagate(): step_size * jnp.stack([real_rate, imag_rate], axis=1)  50.1 us
    concatenate x16, local copies, waits for them, and re-layouts, propagate(): jnp.roll(real_part, -1, axis=-1)  49.4 us
    all_gather x1, waiting for transfers between devices, shards(): totals = lax.all_gather(group_product[None], 'grp', axis=0, tiled=True)  49.3 us
    psum x1, waiting for transfers between devices, broadcast(): return lax.psum(jnp.where(mine, x, jnp.zeros_like(x)), axis)  45.2 us
  transfers between devices with their start and end apart: 5, of which 5 were waited for; matrix products, arithmetic and copies ran while one was open for 0% of the time, Pallas kernels for 0%

commit v1 on v0

v1 whole, which is shorter than its diff:
```python
import jax
import jax.numpy as jnp
from jax import lax
from jax.experimental import pallas as pl
from jax.experimental.pallas import tpu as pltpu
from jax.sharding import PartitionSpec as P

HI = lax.Precision.HIGHEST
GROUP = 16


def split3(x):
    hi = x.astype(jnp.bfloat16)
    rest = x - hi.astype(jnp.float32)
    mid = rest.astype(jnp.bfloat16)
    low = (rest - mid.astype(jnp.float32)).astype(jnp.bfloat16)
    return hi, mid, low


def left6(x):
    h, m, l = split3(x)
    return jnp.concatenate([h, h, m, m, h, l], axis=1)


def right6(x):
    h, m, l = split3(x)
    return jnp.concatenate([h, m, h, m, l, h], axis=0)


def mm(a, b):
    return jnp.dot(left6(a), right6(b), preferred_element_type=jnp.float32)


def _transfer_kernel(nbr, steps, det, disp, basis, bg, out, perm, co, w0, w1, bc, pr, acc):
    g = pl.program_id(0)
    last = pl.num_programs(0) - 1
    vecs, cycles, samples = bc.shape[2], bc.shape[1], bc.shape[3]

    @pl.when(g == 0)
    def _():
        i = lax.broadcasted_iota(jnp.int32, (256, 256), 0)
        j = lax.broadcasted_iota(jnp.int32, (256, 256), 1)
        hit = jnp.logical_and(i // 16 == j % 16, i % 16 == j // 16)
        perm[...] = jnp.where(hit, 1.0, 0.0).astype(jnp.bfloat16)

        @pl.loop(0, cycles)
        def _(r):
            for t in range(2):
                a = bg[t, 0, pl.ds(r, 1), :]
                b = bg[t, 1, pl.ds(r, 1), :]
                inten = 2.0 * (a * a + b * b)
                p = a * a - b * b
                q = 2.0 * a * b
                lin = (det[r] + 2.0 * disp[r]) - inten
                for k, val in enumerate((9.0 - q, lin + p, 9.0 + q, p - lin)):
                    co[t, k, r] = jnp.broadcast_to(val, (8, samples))

    for p in range(2):
        for h in range(cycles // 16):
            for nb in range(samples // 256):
                x = basis[:, p, h * 16:(h + 1) * 16, nb * 256:(nb + 1) * 256].reshape(256, 256)
                y = jnp.dot(perm[...], x, preferred_element_type=jnp.float32).reshape(16, 16, 256)
                w0[p, h * 16:(h + 1) * 16, :, nb * 256:(nb + 1) * 256] = y
                bc[p, h * 16:(h + 1) * 16, pl.ds(g * GROUP, GROUP), nb * 256:(nb + 1) * 256] = y.astype(jnp.bfloat16)

    def advance(src, t, r, lo):
        n0, n1 = nbr[r, 0], nbr[r, 1]
        vs = slice(lo, lo + 8)
        beta = disp[r]
        u, v = src[0, r, vs, :], src[1, r, vs, :]
        cu = src[0, n0, vs, :] + src[0, n1, vs, :]
        cv = src[1, n0, vs, :] + src[1, n1, vs, :]
        su = pltpu.roll(u, 1, 1) + pltpu.roll(u, samples - 1, 1)
        sv = pltpu.roll(v, 1, 1) + pltpu.roll(v, samples - 1, 1)
        nu = (co[t, 0, r] * u + co[t, 1, r] * v) - (beta * sv + cv)
        nv = (co[t, 2, r] * v + co[t, 3, r] * u) + (beta * su + cu)
        return nu, nv

    @pl.loop(0, cycles)
    def _(r):
        for lo in range(0, GROUP, 8):
            nu, nv = advance(w0, 0, r, lo)
            w1[0, r, lo:lo + 8, :] = nu
            w1[1, r, lo:lo + 8, :] = nv

    rows = pl.ds(pl.multiple_of(g * GROUP, GROUP), GROUP)

    @pl.when(steps[0] >= 2)
    def _():
        @pl.loop(0, cycles)
        def _(r):
            res = [advance(w1, 1, r, lo) for lo in range(0, GROUP, 8)]
            for p in range(2):
                full = jnp.concatenate([0.01 * x[p] for x in res], axis=0)
                pr[p, r, rows, :] = full.astype(jnp.bfloat16)

    @pl.when(steps[0] < 2)
    def _():
        @pl.loop(0, cycles)
        def _(r):
            for p in range(2):
                pr[p, r, rows, :] = (0.1 * w1[p, r]).astype(jnp.bfloat16)

    @pl.when(g == last)
    def _():
        acc[...] = jnp.zeros_like(acc)

        @pl.loop(0, cycles)
        def _(r):
            tot = acc[...]
            for p in range(2):
                tot += lax.dot_general(bc[p, r], pr[p, r], (((1,), (1,)), ((), ())),
                                       preferred_element_type=jnp.float32)
            acc[...] = tot

        proj = acc[...]
        gen = 0.25 * (proj - proj.T)
        i = lax.broadcasted_iota(jnp.int32, (vecs, vecs), 0)
        j = lax.broadcasted_iota(jnp.int32, (vecs, vecs), 1)
        eye = jnp.where(i == j, 1.0, 0.0)
        gram = -mm(gen, gen)
        bound = jnp.max(jnp.sum(jnp.abs(gram), axis=0))
        scale = 2.0 / (2.0 + bound)
        resid = eye - scale * (eye + gram)
        prod = scale * (eye + 2.0 * gen - gram)

        def more(c):
            return c[0] > 1e-7

        def body(c):
            rho, rs, pd = c
            return (rho * rho,
                    mm(rs, rs),
                    pd + mm(rs, pd))

        out[...] = lax.while_loop(more, body, (0.5 * bound * scale, resid, prod))[2]


def segment_transfer(basis, bg, det, disp, nbr, steps):
    vecs, _, cycles, samples = basis.shape
    smem = pl.BlockSpec(memory_space=pltpu.SMEM)
    return pl.pallas_call(
        _transfer_kernel,
        grid=(vecs // GROUP,),
        out_shape=jax.ShapeDtypeStruct((vecs, vecs), jnp.float32),
        in_specs=[smem, smem, smem, smem,
                  pl.BlockSpec((GROUP, 2, cycles, samples), lambda g: (g, 0, 0, 0)),
                  pl.BlockSpec(memory_space=pltpu.VMEM)],
        out_specs=pl.BlockSpec((vecs, vecs), lambda g: (0, 0)),
        scratch_shapes=[
            pltpu.VMEM((256, 256), jnp.bfloat16),
            pltpu.VMEM((2, 4, cycles, 8, samples), jnp.float32),
            pltpu.VMEM((2, cycles, GROUP, samples), jnp.float32),
            pltpu.VMEM((2, cycles, GROUP, samples), jnp.float32),
            pltpu.VMEM((2, cycles, vecs, samples), jnp.bfloat16),
            pltpu.VMEM((2, cycles, vecs, samples), jnp.bfloat16),
            pltpu.VMEM((vecs, vecs), jnp.float32),
        ],
        compiler_params=pltpu.CompilerParams(vmem_limit_bytes=60 * 1024 * 1024),
        name="segment_transfer",
    )(nbr, steps, det, disp, basis, bg)


def shifted_2(value, axis, steps):
    count = lax.axis_size(axis)
    first, last = (max(0, -steps), min(count, count - steps))
    return lax.ppermute(value, axis, [(source, source + steps) for source in range(first, last)])


def broadcast(x, axis, root):
    mine = lax.axis_index(axis) == root
    return lax.psum(jnp.where(mine, x, jnp.zeros_like(x)), axis)


def compose(latter, former):
    return jnp.dot(latter, former, precision=lax.Precision.HIGHEST)


def batch_compose(former, latter):
    return jnp.einsum("bij,bjk->bik", latter, former, precision=lax.Precision.HIGHEST)


def shards(basis, background, detuning, dispersion, neighbors, step_counts):
    vec_count = basis.shape[0]
    transfer = segment_transfer(
        basis, background[0, 0], detuning, dispersion, neighbors, step_counts.reshape(1)
    )
    identity = jnp.eye(vec_count, dtype=jnp.float32)
    seq_count = lax.axis_size("seq")
    seq_pos = lax.axis_index("seq")
    before = identity
    through = transfer
    for hop_index in range(1, seq_count):
        arrived = shifted_2(through, "seq", 1)
        is_mine = seq_pos == hop_index
        before = jnp.where(is_mine, arrived, before)
        through = jnp.where(is_mine, compose(transfer, arrived), through)
    group_product = broadcast(through, "seq", seq_count - 1)
    grp_count = lax.axis_size("grp")
    grp_pos = lax.axis_index("grp")
    totals = lax.all_gather(group_product[None], "grp", axis=0, tiled=True)
    running = lax.associative_scan(batch_compose, totals)
    monodromy = running[grp_count - 1]
    shifted = jnp.concatenate([identity[None], running[:-1]], axis=0)
    earlier = lax.dynamic_index_in_dim(shifted, grp_pos, 0, keepdims=False)
    prefix = compose(before, earlier)
    return (prefix[None, None], monodromy)


def solution(mesh):
    in_specs = (P(), P("grp", "seq", None, None, None, None), P(), P(), P(), P("grp", "seq"))
    out_specs = (P("grp", "seq", None, None), P())
    return jax.shard_map(shards, mesh=mesh, in_specs=in_specs, out_specs=out_specs, check_vma=False)
```

time: 728 us -> 257 us (0.35)
  other arithmetic: 214 us -> 3.67 us
  local copies, waits for them, and re-layouts: 215 us -> 20.9 us
  matrix products: 161 us -> 12.3 us
  Pallas kernels: 0 us -> 94.1 us
  loops' own time: 9.17 us -> 0 us
    dot_general x14 -> x0, matrix products: 151 us -> none  [the longest x8 86.4 us: propagate(): jnp.einsum('rm,bcmn->bcrn', coupling, field_state, precision=lax.Precisio...]
    sub x9 -> x0, other arithmetic: 107 us -> none  [the longest x8 105 us: propagate(): -real_part + detune_col * imag_part - disp_col * lap_im]
    pallas_call x0 -> x1, Pallas kernels: none -> 94.1 us  [segment_transfer(): pl.pallas_call(_transfer_kernel, grid=(vecs // GROUP,), out_shape=jax.Sha...]
    concatenate x24 -> x0, local copies, waits for them, and re-layouts: 68.7 us -> none  [the longest x16 49.4 us: propagate(): jnp.roll(real_part, -1, axis=-1)]
    while x56 -> x0, local copies, waits for them, and re-layouts: 64.8 us -> none
    mul x17 -> x0, other arithmetic: 52.9 us -> none  [the longest x8 50.1 us: propagate(): step_size * jnp.stack([real_rate, imag_rate], axis=1)]
    convert_element_type x4 -> x0, local copies, waits for them, and re-layouts: 29.9 us -> none  [one_block(): vec_block.astype(jnp.float32)]
    convert_element_type x5 -> x1, other arithmetic: 27.4 us -> 0.01 us  [shards(): identity = jnp.eye(vec_count, dtype=jnp.float32)]
where the time goes in v1:
time: 257 us; the launch traced here: 256 us
  waiting for transfers between devices  100 us (39%)
  Pallas kernels  94.1 us (37%)
  local copies, waits for them, and re-layouts  20.9 us (8%)
  between operations  15 us (6%)
  matrix products  12.3 us (5%)
  starting transfers between devices  10.2 us (4%)
  other arithmetic  3.67 us (1%)
    pallas_call x1, Pallas kernels, segment_transfer(): pl.pallas_call(_transfer_kernel, grid=(vecs // GROUP,), out_shape=jax.Sha...  94.1 us
    all_gather x1, waiting for transfers between devices, shards(): totals = lax.all_gather(group_product[None], 'grp', axis=0, tiled=True)  49.3 us
    psum x1, waiting for transfers between devices, broadcast(): return lax.psum(jnp.where(mine, x, jnp.zeros_like(x)), axis)  46.5 us
    pad x8, local copies, waits for them, and re-layouts, shards(): running = lax.associative_scan(batch_compose, totals)  13.2 us
    ppermute x3, starting transfers between devices, shifted_2(): lax.ppermute(value, axis, [(source, source + steps) for source in range(f...  10.1 us
    unnamed x4, local copies, waits for them, and re-layouts  7.71 us
    dot_general x9, matrix products, batch_compose(): jnp.einsum('bij,bjk->bik', latter, former, precision=lax.Precision.HIGHEST)  7.62 us
  transfers between devices with their start and end apart: 5, of which 5 were waited for; matrix products, arithmetic and copies ran while one was open for 0% of the time, Pallas kernels for 0%

profile of v1, /device:TPU:1, one launch (start us, length us, event | category | flops | bytes accessed | tf_op | source)
XLA Modules:
  0.0 256.2 jit_solution(9788123711544761709)
XLA Ops:
  7.2 0.0 all-reduce.12.cloned.1.call-start
  7.9 1.4 copy.9.nbr
  9.2 94.1 %segment_transfer.1 = f32[128,128]{1,0:T(8,128)} custom-call(s32[32,2]{1,0:T(8,128)} %copy.9.nbr, s32[1]{0:T(128)} %bitcast.33.steps, f32[32]{0:T(128)} %det.1, f32[32]{0:T(128)} %disp.1, bf16[128,2,32,1024]{3,2,1,0:T(8,128)(2,1)} %basis.1, f32[2,2,32,1024]{3,2,1,0:T(8,128)} %bitcast.34), custom_call_target="tpu_custom_call" | custom-call | tf_op jit(solution)/shard_map/segment_transfer/pallas_call | solution.py:142
  103.3 1.3 collective-permute-start
  104.6 1.6 collective-permute-done
  106.3 1.1 convolution_select_fusion
  107.4 3.6 %collective-permute-start.1 = (f32[128,128]{1,0:T(8,128)S(1)}, f32[128,128]{1,0:T(8,128)S(1)}, u32[]{:S(2)}, u32[]{:S(2)}) collective-permute-start(f32[128,128]{1,0:T(8,128)S(1)} %convolution_select_fusion), channel_id=1, source_target_pairs={{0,32},{32,64},{64,96},{1,33},{33,65},{65,97},{2,34},{34,66},{66,9... | collective-permute-start | bytes 196616 | tf_op jit(solution)/shard_map/ppermute | solution.py:167
  111.0 1.3 collective-permute-done.1
  112.3 1.0 convolution_select_fusion.2
  113.3 5.3 %collective-permute-start.2 = (f32[128,128]{1,0:T(8,128)S(1)}, f32[128,128]{1,0:T(8,128)S(1)}, u32[]{:S(2)}, u32[]{:S(2)}) collective-permute-start(f32[128,128]{1,0:T(8,128)S(1)} %convolution_select_fusion.2), channel_id=1, source_target_pairs={{0,32},{32,64},{64,96},{1,33},{33,65},{65,97},{2,34},{34,66},{66,9... | collective-permute-start | bytes 196616 | tf_op jit(solution)/shard_map/ppermute | solution.py:167
  118.6 1.3 collective-permute-done.2
  119.9 1.7 fusion.1
  121.6 0.0 all-reduce.12.cloned.1.call-update
  121.6 0.0 all-gather.2.cloned.1.call-start
  121.7 46.5 %all-reduce.12.cloned.1.call-done = f32[1,128,128]{2,1,0:T(8,128)} async-done(((f32[1,128,128]{2,1,0:T(8,128)}), f32[1,128,128]{2,1,0:T(8,128)}) %all-reduce.12.cloned.1.call-update) | async-done | bytes 65552 | tf_op jit(solution)/shard_map/psum | solution.py:172
  168.2 0.0 all-gather.2.cloned.1.call-update
  168.2 49.3 %all-gather.2.cloned.1.call-done = f32[32,128,128]{2,1,0:T(8,128)} async-done(((f32[1,128,128]{2,1,0:T(8,128)}), f32[32,128,128]{2,1,0:T(8,128)}) %all-gather.2.cloned.1.call-update) | async-done | bytes 2097168 | tf_op jit(solution)/shard_map/all_gather | solution.py:201
  217.5 2.7 %fusion.2 = f32[16,128,128]{2,1,0:T(8,128)S(1)} fusion(f32[32,128,128]{2,1,0:T(8,128)} %all-gather.2.cloned.1.call-done), kind=kOutput, calls=%fused_computation.12 | convolution fusion | flops 402653184 | bytes 3145728 | tf_op jit(solution)/shard_map/bij,bjk->bik/dot_general | solution.py:180
  220.2 0.6 fusion.10
  220.9 0.4 fusion.18
  221.3 0.3 fusion.26
  221.6 0.2 convolution_bitcast_fusion.2
  221.8 0.2 convolution_bitcast_fusion.1
  222.1 0.3 fusion.21
  222.5 0.1 pad.35
  222.6 0.1 pad.36
  222.7 0.6 fusion.13
  223.2 0.1 add.43
  223.4 0.1 pad.37
  223.5 0.1 pad.38
  223.6 0.1 add.44
  223.8 6.3 %pad.87 = f32[31,128,128]{2,1,0:T(8,128)} pad(f32[16,128,128]{2,1,0:T(8,128)S(1)} %add.44, f32[]{:T(128)} %constant.20.clone.1), padding=0_0_1x0_0_0x0_0_0 | pad | bytes 3080196
  230.1 6.3 %pad.40 = f32[32,128,128]{2,1,0:T(8,128)} pad(f32[16,128,128]{2,1,0:T(8,128)S(1)} %add.44, f32[]{:T(128)} %constant.20.clone.1), padding=1_0_1x0_0_0x0_0_0 | pad | bytes 3145732 | tf_op jit(solution)/shard_map/pad | solution.py:202
  236.5 0.0 slice-start
  236.5 2.3 fusion.5
  238.8 0.0 slice-done
  238.8 0.1 pad_maximum_fusion
  238.9 0.0 copy-start
  238.9 6.4 %pad.39 = f32[32,128,128]{2,1,0:T(8,128)} pad(f32[16,128,128]{2,1,0:T(8,128)S(1)} %pad_maximum_fusion, f32[]{:T(128)} %constant.20.clone.1), padding=0_1_1x0_0_0x0_0_0 | pad | bytes 3145732 | tf_op jit(solution)/shard_map/pad | solution.py:202
  245.3 1.5 add_bitcast_fusion
  246.7 0.0 copy-done
  246.7 1.8 slice_add_fusion
  248.5 0.9 convolution_bitcast_fusion
  (12 shorter events, 0.2 us)
Async XLA Ops:
  7.2 161.0 %all-reduce.12.cloned.1.call-start = ((), (), s32[]{:S(2)}) async-start(), calls=%async_computation | async-start | bytes 131072 | tf_op jit(solution)/shard_map/psum | solution.py:172
  103.3 2.9 %collective-permute-start = (f32[128,128]{1,0:T(8,128)}, f32[128,128]{1,0:T(8,128)S(1)}, u32[]{:S(2)}, u32[]{:S(2)}) collective-permute-start(f32[128,128]{1,0:T(8,128)} %segment_transfer.1), channel_id=1, source_target_pairs={{0,32},{32,64},{64,96},{1,33},{33,65},{65,97},{2,34},{34,66},{66,9... | collective-permute-start | bytes 196616 | tf_op jit(solution)/shard_map/ppermute | solution.py:167
  107.4 4.9 %collective-permute-start.1 = (f32[128,128]{1,0:T(8,128)S(1)}, f32[128,128]{1,0:T(8,128)S(1)}, u32[]{:S(2)}, u32[]{:S(2)}) collective-permute-start(f32[128,128]{1,0:T(8,128)S(1)} %convolution_select_fusion), channel_id=1, source_target_pairs={{0,32},{32,64},{64,96},{1,33},{33,65},{65,97},{2,34},{34,66},{66,9... | collective-permute-start | bytes 196616 | tf_op jit(solution)/shard_map/ppermute | solution.py:167
  113.3 6.6 %collective-permute-start.2 = (f32[128,128]{1,0:T(8,128)S(1)}, f32[128,128]{1,0:T(8,128)S(1)}, u32[]{:S(2)}, u32[]{:S(2)}) collective-permute-start(f32[128,128]{1,0:T(8,128)S(1)} %convolution_select_fusion.2), channel_id=1, source_target_pairs={{0,32},{32,64},{64,96},{1,33},{33,65},{65,97},{2,34},{34,66},{66,9... | collective-permute-start | bytes 196616 | tf_op jit(solution)/shard_map/ppermute | solution.py:167
  121.6 95.9 %all-gather.2.cloned.1.call-start = ((), (), s32[]{:S(2)}) async-start(), calls=%async_computation.1 | async-start | bytes 2162688 | tf_op jit(solution)/shard_map/all_gather | solution.py:201
  236.5 2.3 slice-start
  238.9 7.9 %copy-start = (f32[32,128,128]{2,1,0:T(8,128)S(1)}, f32[32,128,128]{2,1,0:T(8,128)}, u32[]{:S(2)}) copy-start(f32[32,128,128]{2,1,0:T(8,128)} %pad.40) | copy-start | bytes 6291460
Sparse Core Ops, SparseCore 0:
  121.7 46.3 all-reduce.11
  170.7 46.7 all-gather.1

commit v2 on v1

--- a/solution.py
+++ b/solution.py
@@ -1,3 +1,4 @@
+import functools
 import jax
 import jax.numpy as jnp
 from jax import lax
@@ -161,49 +162,107 @@
     )(nbr, steps, det, disp, basis, bg)
 
 
-def shifted_2(value, axis, steps):
-    count = lax.axis_size(axis)
-    first, last = (max(0, -steps), min(count, count - steps))
-    return lax.ppermute(value, axis, [(source, source + steps) for source in range(first, last)])
-
-
-def broadcast(x, axis, root):
-    mine = lax.axis_index(axis) == root
-    return lax.psum(jnp.where(mine, x, jnp.zeros_like(x)), axis)
-
-
-def compose(latter, former):
-    return jnp.dot(latter, former, precision=lax.Precision.HIGHEST)
-
-
-def batch_compose(former, latter):
-    return jnp.einsum("bij,bjk->bik", latter, former, precision=lax.Precision.HIGHEST)
-
+def split2(x):
+    hi = x.astype(jnp.bfloat16)
+    return hi, (x - hi.astype(jnp.float32)).astype(jnp.bfloat16)
+
+
+def mm3(a, b):
+    ah, al = split2(a)
+    bh, bl = split2(b)
+    return jnp.dot(jnp.concatenate([ah, ah, al], axis=1), jnp.concatenate([bh, bl, bh], axis=0),
+                   preferred_element_type=jnp.float32)
+
+
+def _chain_kernel(t_ref, pre_ref, mono_ref, slots, pair, low, before, send_sem, recv_sem):
+    seq, grp = lax.axis_index("seq"), lax.axis_index("grp")
+    core = lax.rem(grp, 2)
+    depth = lax.rem(lax.div(grp, 2), 4)
+    wide = lax.div(grp, 8)
+    rounds = (
+        (4, seq, lambda pos: (pos, grp)),
+        (2, core, lambda pos: (seq, grp - core + pos)),
+        (4, depth, lambda pos: (seq, grp + (pos - depth) * 2)),
+        (4, wide, lambda pos: (seq, grp + (pos - wide) * 8)),
+    )
+    mesh_id = pl.DeviceIdType.MESH
+    barrier = pltpu.get_barrier_semaphore()
+    for radix, pos, place in rounds:
+        for hop in range(1, radix):
+            pl.semaphore_signal(barrier, inc=1, device_id=place(lax.rem(pos + hop, radix)), device_id_type=mesh_id)
+    pl.semaphore_wait(barrier, sum(r[0] - 1 for r in rounds))
+
+    def prefix_step(k, last):
+        radix, pos, _ = rounds[k]
+
+        @pl.when(pos == 1)
+        def _():
+            before[...] = slots[k, 0] if k == 0 else mm3(before[...], slots[k, 0])
+
+        if radix == 4:
+            @pl.when(pos == 2)
+            def _():
+                before[...] = low[...] if k == 0 else mm3(before[...], low[...])
+
+            @pl.when(pos == 3)
+            def _():
+                left = slots[k, 2] if k == 0 else mm3(before[...], slots[k, 2])
+                before[...] = mm3(left, low[...])
+
+    n = t_ref.shape[0]
+    i = lax.broadcasted_iota(jnp.int32, (n, n), 0)
+    j = lax.broadcasted_iota(jnp.int32, (n, n), 1)
+    before[...] = jnp.where(i == j, 1.0, 0.0)
+    sends = []
+    own = t_ref
+    for k, (radix, pos, place) in enumerate(rounds):
+        copies = []
+        for hop in ((2, 1, 3) if radix == 4 else (1,)):
+            copy = pltpu.make_async_remote_copy(
+                src_ref=own, dst_ref=slots.at[k, pos], send_sem=send_sem.at[k, hop], recv_sem=recv_sem.at[k, hop],
+                device_id=place(lax.rem(pos + hop, radix)), device_id_type=mesh_id)
+            copy.start()
+            copies.append(copy)
+        sends += copies
+        slots[k, pos] = own[...]
+        if k:
+            prefix_step(k - 1, False)
+        for copy in copies:
+            copy.wait_recv()
+        if radix == 4:
+            first = mm3(slots[k, 1], slots[k, 0])
+            low[...] = first
+            total = mm3(mm3(slots[k, 3], slots[k, 2]), first)
+        else:
+            total = mm3(slots[k, 1], slots[k, 0])
+        if k + 1 < len(rounds):
+            pair[k] = total
+            own = pair.at[k]
+        else:
+            mono_ref[...] = total
+    prefix_step(len(rounds) - 1, True)
+    pre_ref[...] = before[...]
+    for copy in sends:
+        copy.wait_send()
+
+
+def chain(t):
+    n = t.shape[0]
+    shape = jax.ShapeDtypeStruct((n, n), jnp.float32)
+    vm = pl.BlockSpec(memory_space=pltpu.VMEM)
+    return pl.pallas_call(
+        _chain_kernel, out_shape=(shape, shape), in_specs=[vm], out_specs=(vm, vm),
+        scratch_shapes=[pltpu.VMEM((4, 4, n, n), jnp.float32), pltpu.VMEM((3, n, n), jnp.float32),
+                        pltpu.VMEM((n, n), jnp.float32), pltpu.VMEM((n, n), jnp.float32),
+                        pltpu.SemaphoreType.DMA((4, 4)), pltpu.SemaphoreType.DMA((4, 4))],
+        compiler_params=pltpu.CompilerParams(collective_id=0, has_side_effects=True),
+        name="chain_products")(t)
 
 def shards(basis, background, detuning, dispersion, neighbors, step_counts):
-    vec_count = basis.shape[0]
-    transfer = segment_transfer(
+    own = segment_transfer(
         basis, background[0, 0], detuning, dispersion, neighbors, step_counts.reshape(1)
     )
-    identity = jnp.eye(vec_count, dtype=jnp.float32)
-    seq_count = lax.axis_size("seq")
-    seq_pos = lax.axis_index("seq")
-    before = identity
-    through = transfer
-    for hop_index in range(1, seq_count):
-        arrived = shifted_2(through, "seq", 1)
-        is_mine = seq_pos == hop_index
-        before = jnp.where(is_mine, arrived, before)
-        through = jnp.where(is_mine, compose(transfer, arrived), through)
-    group_product = broadcast(through, "seq", seq_count - 1)
-    grp_count = lax.axis_size("grp")
-    grp_pos = lax.axis_index("grp")
-    totals = lax.all_gather(group_product[None], "grp", axis=0, tiled=True)
-    running = lax.associative_scan(batch_compose, totals)
-    monodromy = running[grp_count - 1]
-    shifted = jnp.concatenate([identity[None], running[:-1]], axis=0)
-    earlier = lax.dynamic_index_in_dim(shifted, grp_pos, 0, keepdims=False)
-    prefix = compose(before, earlier)
+    prefix, monodromy = chain(own)
     return (prefix[None, None], monodromy)
 
 

time: 257 us -> 126 us (0.49)
  waiting for transfers between devices: 100 us -> 0 us
  Pallas kernels: 94.1 us -> 121 us
  local copies, waits for them, and re-layouts: 20.9 us -> 4.31 us
  between operations: 15 us -> 1.29 us
  matrix products: 12.3 us -> 0 us
  starting transfers between devices: 10.2 us -> 0 us
  other arithmetic: 3.67 us -> 0 us
    all_gather x1 -> x0, waiting for transfers between devices: 49.3 us -> none  [shards(): totals = lax.all_gather(group_product[None], 'grp', axis=0, tiled=True)]
    psum x1 -> x0, waiting for transfers between devices: 46.5 us -> none  [broadcast(): return lax.psum(jnp.where(mine, x, jnp.zeros_like(x)), axis)]
    pallas_call x0 -> x1, Pallas kernels: none -> 26.2 us  [chain(): pl.pallas_call(_chain_kernel, out_shape=(shape, shape), in_specs=[vm], ou...]
    pad x8 -> x0, local copies, waits for them, and re-layouts: 13.2 us -> none  [shards(): running = lax.associative_scan(batch_compose, totals)]
    dot_general x13 -> x0, matrix products: 12.3 us -> none  [the longest x9 7.62 us: batch_compose(): jnp.einsum('bij,bjk->bik', latter, former, precision=lax.Precision.HIGHEST)]
    ppermute x3 -> x0, starting transfers between devices: 10.1 us -> none  [shifted_2(): lax.ppermute(value, axis, [(source, source + steps) for source in range(f...]
    ppermute x3 -> x0, waiting for transfers between devices: 4.23 us -> none  [shifted_2(): lax.ppermute(value, axis, [(source, source + steps) for source in range(f...]
    unnamed x4 -> x3, local copies, waits for them, and re-layouts: 7.71 us -> 4.31 us
  transfers between devices with their start and end apart: 5 -> 0, of which waited for: 5 -> 0; matrix products, arithmetic and copies ran while one was open for 0% -> 0% of each run, Pallas kernels for 0% -> 0%
where the time goes in v2:
time: 126 us
  Pallas kernels  121 us (96%)
  local copies, waits for them, and re-layouts  4.31 us (3%)
  between operations  1.29 us (1%)
    pallas_call x1, Pallas kernels, segment_transfer(): pl.pallas_call(_transfer_kernel, grid=(vecs // GROUP,), out_shape=jax.Sha...  94.4 us
    pallas_call x1, Pallas kernels, chain(): pl.pallas_call(_chain_kernel, out_shape=(shape, shape), in_specs=[vm], ou...  26.2 us
    unnamed x3, local copies, waits for them, and re-layouts  4.31 us

profile of v2, /device:TPU:1, one launch (start us, length us, event | category | flops | bytes accessed | tf_op | source)
XLA Modules:
  0.0 126.1 jit_solution(14992931824884076961)
XLA Ops:
  1.3 1.4 %copy.8.nbr = s32[32,2]{1,0:T(8,128)} copy(s32[32,2]{0,1:T(2,128)} %param.10) | data formatting | bytes 512 | tf_op args[4]
  2.6 94.4 %segment_transfer.1.t_ref = f32[128,128]{1,0:T(8,128)} custom-call(s32[32,2]{1,0:T(8,128)} %copy.8.nbr, s32[1]{0:T(128)} %bitcast.3.steps, f32[32]{0:T(128)} %det.1, f32[32]{0:T(128)} %disp.1, bf16[128,2,32,1024]{3,2,1,0:T(8,128)(2,1)} %basis.1, f32[2,2,32,1024]{3,2,1,0:T(8,128)} %bitcast.4), custom_call_target="tpu_custom_call" | custom-call | tf_op jit(solution)/shard_map/segment_transfer/pallas_call | solution.py:143
  97.0 26.2 %chain_products.1 = (f32[128,128]{1,0:T(8,128)}, f32[128,128]{1,0:T(8,128)}) custom-call(f32[128,128]{1,0:T(8,128)} %segment_transfer.1.t_ref), custom_call_target="tpu_custom_call" | custom-call | tf_op jit(solution)/shard_map/chain_products/pallas_call | solution.py:253
  123.2 1.5 %copy.12 = f32[1,1,128,128]{3,2,1,0:T(8,128)} copy(f32[1,1,128,128]{3,2,1,0:T(8,128)} %bitcast.5) | data formatting | bytes 131072
  124.7 1.5 %copy.13 = f32[128,128]{1,0:T(8,128)} copy(f32[128,128]{1,0:T(8,128)} %get-tuple-element.9) | data formatting | bytes 131072

commit v3 on v2

--- a/solution.py
+++ b/solution.py
@@ -64,36 +64,47 @@
                 w0[p, h * 16:(h + 1) * 16, :, nb * 256:(nb + 1) * 256] = y
                 bc[p, h * 16:(h + 1) * 16, pl.ds(g * GROUP, GROUP), nb * 256:(nb + 1) * 256] = y.astype(jnp.bfloat16)
 
+    def around(x):
+        lane = lax.broadcasted_iota(jnp.int32, (8, 128), 1)
+        first, final = lane == 0, lane == 127
+        cols = [x[:, 128 * j:128 * j + 128] for j in range(samples // 128)]
+        n = len(cols)
+        down = [pltpu.roll(c, 1, 1) for c in cols]
+        up = [pltpu.roll(c, 127, 1) for c in cols]
+        return jnp.concatenate([jnp.where(first, down[j - 1], down[j]) + jnp.where(final, up[(j + 1) % n], up[j]) for j in range(n)], axis=1)
+
     def advance(src, t, r, lo):
-        n0, n1 = nbr[r, 0], nbr[r, 1]
+        n0, n1 = nbr[0, r], nbr[1, r]
         vs = slice(lo, lo + 8)
         beta = disp[r]
         u, v = src[0, r, vs, :], src[1, r, vs, :]
         cu = src[0, n0, vs, :] + src[0, n1, vs, :]
         cv = src[1, n0, vs, :] + src[1, n1, vs, :]
-        su = pltpu.roll(u, 1, 1) + pltpu.roll(u, samples - 1, 1)
-        sv = pltpu.roll(v, 1, 1) + pltpu.roll(v, samples - 1, 1)
+        su = around(u)
+        sv = around(v)
         nu = (co[t, 0, r] * u + co[t, 1, r] * v) - (beta * sv + cv)
         nv = (co[t, 2, r] * v + co[t, 3, r] * u) + (beta * su + cu)
         return nu, nv
 
-    @pl.loop(0, cycles)
-    def _(r):
-        for lo in range(0, GROUP, 8):
-            nu, nv = advance(w0, 0, r, lo)
-            w1[0, r, lo:lo + 8, :] = nu
-            w1[1, r, lo:lo + 8, :] = nv
+    @pl.loop(0, cycles // 8)
+    def _(rr):
+        for r in [rr * 8 + k for k in range(8)]:
+            for lo in range(0, GROUP, 8):
+                nu, nv = advance(w0, 0, r, lo)
+                w1[0, r, lo:lo + 8, :] = nu
+                w1[1, r, lo:lo + 8, :] = nv
 
     rows = pl.ds(pl.multiple_of(g * GROUP, GROUP), GROUP)
 
     @pl.when(steps[0] >= 2)
     def _():
-        @pl.loop(0, cycles)
-        def _(r):
-            res = [advance(w1, 1, r, lo) for lo in range(0, GROUP, 8)]
-            for p in range(2):
-                full = jnp.concatenate([0.01 * x[p] for x in res], axis=0)
-                pr[p, r, rows, :] = full.astype(jnp.bfloat16)
+        @pl.loop(0, cycles // 8)
+        def _(rr):
+            for r in [rr * 8 + k for k in range(8)]:
+                res = [advance(w1, 1, r, lo) for lo in range(0, GROUP, 8)]
+                for p in range(2):
+                    full = jnp.concatenate([0.01 * x[p] for x in res], axis=0)
+                    pr[p, r, rows, :] = full.astype(jnp.bfloat16)
 
     @pl.when(steps[0] < 2)
     def _():
@@ -159,7 +170,7 @@
         ],
         compiler_params=pltpu.CompilerParams(vmem_limit_bytes=60 * 1024 * 1024),
         name="segment_transfer",
-    )(nbr, steps, det, disp, basis, bg)
+    )(nbr.T, steps, det, disp, basis, bg)
 
 
 def split2(x):

time: 126 us -> 90.9 us (0.72)
  Pallas kernels: 121 us -> 86.4 us
  local copies, waits for them, and re-layouts: 4.31 us -> 2.95 us
    pallas_call x1, Pallas kernels: 94.4 us -> 61.4 us  [segment_transfer(): pl.pallas_call(_transfer_kernel, grid=(vecs // GROUP,), out_shape=jax.Sha...]
    unnamed x3 -> x2, local copies, waits for them, and re-layouts: 4.31 us -> 2.95 us
where the time goes in v3:
time: 90.9 us; the launch traced here: 90.6 us
  Pallas kernels  86.4 us (95%)
  local copies, waits for them, and re-layouts  2.95 us (3%)
  between operations  1.29 us (1%)
    pallas_call x1, Pallas kernels, segment_transfer(): pl.pallas_call(_transfer_kernel, grid=(vecs // GROUP,), out_shape=jax.Sha...  61.4 us
    pallas_call x1, Pallas kernels, chain(): pl.pallas_call(_chain_kernel, out_shape=(shape, shape), in_specs=[vm], ou...  25 us
    unnamed x2, local copies, waits for them, and re-layouts  2.95 us

profile of v3, /device:TPU:1, one launch (start us, length us, event | category | flops | bytes accessed | tf_op | source)
XLA Modules:
  0.0 90.6 jit_solution(16273047192894832241)
XLA Ops:
  1.3 61.4 %segment_transfer.1.t_ref = f32[128,128]{1,0:T(8,128)} custom-call(s32[2,32]{1,0:T(2,128)} %bitcast.7, s32[1]{0:T(128)} %bitcast.4.steps, f32[32]{0:T(128)} %det.1, f32[32]{0:T(128)} %disp.1, bf16[128,2,32,1024]{3,2,1,0:T(8,128)(2,1)} %basis.1, f32[2,2,32,1024]{3,2,1,0:T(8,128)} %bitcast.5), custom_call_target="tpu_custom_call" | custom-call | tf_op jit(solution)/shard_map/segment_transfer/pallas_call | solution.py:154
  62.7 25.0 %chain_products.1 = (f32[128,128]{1,0:T(8,128)}, f32[128,128]{1,0:T(8,128)}) custom-call(f32[128,128]{1,0:T(8,128)} %segment_transfer.1.t_ref), custom_call_target="tpu_custom_call" | custom-call | tf_op jit(solution)/shard_map/chain_products/pallas_call | solution.py:264
  87.7 1.5 %copy.11 = f32[1,1,128,128]{3,2,1,0:T(8,128)} copy(f32[1,1,128,128]{3,2,1,0:T(8,128)} %bitcast.6) | data formatting | bytes 131072
  89.1 1.5 %copy.12 = f32[128,128]{1,0:T(8,128)} copy(f32[128,128]{1,0:T(8,128)} %get-tuple-element.9) | data formatting | bytes 131072

commit v4 on v2

--- a/solution.py
+++ b/solution.py
@@ -6,15 +6,16 @@
 from jax.experimental.pallas import tpu as pltpu
 from jax.sharding import PartitionSpec as P
 
-HI = lax.Precision.HIGHEST
 GROUP = 16
+UNROLL = 16
+F32, BF16 = jnp.float32, jnp.bfloat16
 
 
 def split3(x):
-    hi = x.astype(jnp.bfloat16)
-    rest = x - hi.astype(jnp.float32)
-    mid = rest.astype(jnp.bfloat16)
-    low = (rest - mid.astype(jnp.float32)).astype(jnp.bfloat16)
+    hi = x.astype(BF16)
+    rest = x - hi.astype(F32)
+    mid = rest.astype(BF16)
+    low = (rest - mid.astype(F32)).astype(BF16)
     return hi, mid, low
 
 
@@ -29,26 +30,65 @@
 
 
 def mm(a, b):
-    return jnp.dot(left6(a), right6(b), preferred_element_type=jnp.float32)
-
-
-def _transfer_kernel(nbr, steps, det, disp, basis, bg, out, perm, co, w0, w1, bc, pr, acc):
+    return jnp.dot(left6(a), right6(b), preferred_element_type=F32)
+
+
+def _transfer_kernel(nbr, steps, det, disp, basis, first, bg, out, rowp, colp, co, w0, w1, bc, pr, mixed, bgp, acc):
     g = pl.program_id(0)
     last = pl.num_programs(0) - 1
     vecs, cycles, samples = bc.shape[2], bc.shape[1], bc.shape[3]
+    parts = cycles // UNROLL
+    later = jnp.minimum(g + 1, last)
+
+    def turn(left, x):
+        return lax.dot_general(left, x, (((1,), (1,)), ((), ())), preferred_element_type=F32)
+
+    def mix_columns(src, ii):
+      for i in (2 * ii, 2 * ii + 1):
+        cols = pl.ds(pl.multiple_of(i * 256, 256), 256)
+        dest = pl.ds(pl.multiple_of(i * 32, 32), 32)
+        for p in range(2):
+            for h in range(2):
+                y = turn(colp[...], src[:, p, h * 16:(h + 1) * 16, cols].reshape(256, 256))
+                mixed[p, h, :, dest, :] = y.astype(BF16).reshape(8, 32, 256)
+
+    def swap_rows(ii, group):
+      for i in (2 * ii, 2 * ii + 1):
+        cols = pl.ds(pl.multiple_of(i * 256, 256), 256)
+        dest = pl.ds(pl.multiple_of(group * GROUP, GROUP), GROUP)
+        for p in range(2):
+            for h in range(2):
+                y = turn(rowp[...], mixed[p, h, pl.ds(2 * i, 2)].reshape(256, 256)).reshape(16, 16, 256)
+                w0[p, h * 16:(h + 1) * 16, :, cols] = y
+                bc[p, h * 16:(h + 1) * 16, dest, cols] = y.astype(BF16)
 
     @pl.when(g == 0)
     def _():
         i = lax.broadcasted_iota(jnp.int32, (256, 256), 0)
         j = lax.broadcasted_iota(jnp.int32, (256, 256), 1)
         hit = jnp.logical_and(i // 16 == j % 16, i % 16 == j // 16)
-        perm[...] = jnp.where(hit, 1.0, 0.0).astype(jnp.bfloat16)
+        rowp[...] = jnp.where(hit, 1.0, 0.0).astype(BF16)
+        hit = j == 8 * (i % 32) + i // 32
+        colp[...] = jnp.where(hit, 1.0, 0.0).astype(BF16)
+
+        lines = bg.shape[0] * 2 * cycles
+        for n in range(samples // 256):
+            terms = split3(bg[:, :, :, n * 256:(n + 1) * 256].reshape(lines, 256))
+            for k in range(3):
+                y = turn(colp[...], terms[k])
+                mixed[k // 2, k % 2, :, n * 32:(n + 1) * 32, 0:lines] = y.astype(BF16).reshape(8, 32, lines)
+        i = lax.broadcasted_iota(jnp.int32, (lines, 3 * lines), 0)
+        j = lax.broadcasted_iota(jnp.int32, (lines, 3 * lines), 1)
+        same = jnp.where(i == j % lines, 1.0, 0.0).astype(BF16)
+        for n in range(samples // 128):
+            x = jnp.concatenate([mixed[k // 2, k % 2, n, :, 0:lines] for k in range(3)], axis=1)
+            bgp[:, :, :, n * 128:(n + 1) * 128] = turn(same, x).reshape(2, 2, cycles, 128)
 
         @pl.loop(0, cycles)
         def _(r):
             for t in range(2):
-                a = bg[t, 0, pl.ds(r, 1), :]
-                b = bg[t, 1, pl.ds(r, 1), :]
+                a = bgp[t, 0, pl.ds(r, 1), :]
+                b = bgp[t, 1, pl.ds(r, 1), :]
                 inten = 2.0 * (a * a + b * b)
                 p = a * a - b * b
                 q = 2.0 * a * b
@@ -56,62 +96,81 @@
                 for k, val in enumerate((9.0 - q, lin + p, 9.0 + q, p - lin)):
                     co[t, k, r] = jnp.broadcast_to(val, (8, samples))
 
-    for p in range(2):
-        for h in range(cycles // 16):
-            for nb in range(samples // 256):
-                x = basis[:, p, h * 16:(h + 1) * 16, nb * 256:(nb + 1) * 256].reshape(256, 256)
-                y = jnp.dot(perm[...], x, preferred_element_type=jnp.float32).reshape(16, 16, 256)
-                w0[p, h * 16:(h + 1) * 16, :, nb * 256:(nb + 1) * 256] = y
-                bc[p, h * 16:(h + 1) * 16, pl.ds(g * GROUP, GROUP), nb * 256:(nb + 1) * 256] = y.astype(jnp.bfloat16)
-
-    def advance(src, t, r, lo):
-        n0, n1 = nbr[r, 0], nbr[r, 1]
-        vs = slice(lo, lo + 8)
+        @pl.loop(0, parts)
+        def _(i):
+            mix_columns(first, i)
+
+        @pl.loop(0, parts)
+        def _(i):
+            swap_rows(i, 0)
+
+    def around(x):
+        col = [x[:, 128 * k:128 * k + 128] for k in range(8)]
+        col = [pltpu.roll(col[7], 1, 1)] + col + [pltpu.roll(col[0], 127, 1)]
+        return jnp.concatenate([col[k] + col[k + 2] for k in range(8)], axis=1)
+
+    def advance(src, t, r):
+        n0, n1 = nbr[0, r], nbr[1, r]
         beta = disp[r]
-        u, v = src[0, r, vs, :], src[1, r, vs, :]
-        cu = src[0, n0, vs, :] + src[0, n1, vs, :]
-        cv = src[1, n0, vs, :] + src[1, n1, vs, :]
-        su = pltpu.roll(u, 1, 1) + pltpu.roll(u, samples - 1, 1)
-        sv = pltpu.roll(v, 1, 1) + pltpu.roll(v, samples - 1, 1)
-        nu = (co[t, 0, r] * u + co[t, 1, r] * v) - (beta * sv + cv)
-        nv = (co[t, 2, r] * v + co[t, 3, r] * u) + (beta * su + cu)
-        return nu, nv
-
-    @pl.loop(0, cycles)
-    def _(r):
-        for lo in range(0, GROUP, 8):
-            nu, nv = advance(w0, 0, r, lo)
-            w1[0, r, lo:lo + 8, :] = nu
-            w1[1, r, lo:lo + 8, :] = nv
+        halves = [slice(lo, lo + 8) for lo in range(0, GROUP, 8)]
+        us = [src[0, r, vs, :] for vs in halves]
+        vs_ = [src[1, r, vs, :] for vs in halves]
+        au = [around(x) for x in us]
+        av = [around(x) for x in vs_]
+        res = ([[], []], [[], []])
+        for k in range(samples // 128):
+            lane = slice(128 * k, 128 * k + 128)
+            c0, c1, c2, c3 = (co[t, m, r, :, lane] for m in range(4))
+            for h, vs in enumerate(halves):
+                u, v = us[h][:, lane], vs_[h][:, lane]
+                cu = src[0, n0, vs, lane] + src[0, n1, vs, lane]
+                cv = src[1, n0, vs, lane] + src[1, n1, vs, lane]
+                res[0][h].append((c0 * u + c1 * v) - (beta * av[h][:, lane] + cv))
+                res[1][h].append((c2 * v + c3 * u) + (beta * au[h][:, lane] + cu))
+        return [[jnp.concatenate(x, axis=1) for x in p] for p in res]
+
+    @pl.loop(0, parts)
+    def _(i):
+        mix_columns(basis, i)
+        for r in [i * UNROLL + k for k in range(UNROLL)]:
+            new = advance(w0, 0, r)
+            for p in range(2):
+                for h in range(2):
+                    w1[p, r, 8 * h:8 * h + 8, :] = new[p][h]
 
     rows = pl.ds(pl.multiple_of(g * GROUP, GROUP), GROUP)
 
     @pl.when(steps[0] >= 2)
     def _():
-        @pl.loop(0, cycles)
-        def _(r):
-            res = [advance(w1, 1, r, lo) for lo in range(0, GROUP, 8)]
-            for p in range(2):
-                full = jnp.concatenate([0.01 * x[p] for x in res], axis=0)
-                pr[p, r, rows, :] = full.astype(jnp.bfloat16)
+        @pl.loop(0, parts)
+        def _(i):
+            swap_rows(i, later)
+            for r in [i * UNROLL + k for k in range(UNROLL)]:
+                new = advance(w1, 1, r)
+                for p in range(2):
+                    full = jnp.concatenate([0.01 * x for x in new[p]], axis=0)
+                    pr[p, r, rows, :] = full.astype(BF16)
 
     @pl.when(steps[0] < 2)
     def _():
-        @pl.loop(0, cycles)
-        def _(r):
-            for p in range(2):
-                pr[p, r, rows, :] = (0.1 * w1[p, r]).astype(jnp.bfloat16)
+        @pl.loop(0, parts)
+        def _(i):
+            swap_rows(i, later)
+            for r in [i * UNROLL + k for k in range(UNROLL)]:
+                for p in range(2):
+                    pr[p, r, rows, :] = (0.1 * w1[p, r]).astype(BF16)
 
     @pl.when(g == last)
     def _():
         acc[...] = jnp.zeros_like(acc)
 
-        @pl.loop(0, cycles)
-        def _(r):
+        @pl.loop(0, parts)
+        def _(i):
             tot = acc[...]
-            for p in range(2):
-                tot += lax.dot_general(bc[p, r], pr[p, r], (((1,), (1,)), ((), ())),
-                                       preferred_element_type=jnp.float32)
+            for k in range(UNROLL):
+                for p in range(2):
+                    tot += lax.dot_general(bc[p, i * UNROLL + k], pr[p, i * UNROLL + k], (((1,), (1,)), ((), ())),
+                                           preferred_element_type=F32)
             acc[...] = tot
 
         proj = acc[...]
@@ -130,9 +189,7 @@
 
         def body(c):
             rho, rs, pd = c
-            return (rho * rho,
-                    mm(rs, rs),
-                    pd + mm(rs, pd))
+            return rho * rho, mm(rs, rs), pd + mm(rs, pd)
 
         out[...] = lax.while_loop(more, body, (0.5 * bound * scale, resid, prod))[2]
 
@@ -140,26 +197,32 @@
 def segment_transfer(basis, bg, det, disp, nbr, steps):
     vecs, _, cycles, samples = basis.shape
     smem = pl.BlockSpec(memory_space=pltpu.SMEM)
+    groups = vecs // GROUP
+    block = (GROUP, 2, cycles, samples)
     return pl.pallas_call(
         _transfer_kernel,
-        grid=(vecs // GROUP,),
-        out_shape=jax.ShapeDtypeStruct((vecs, vecs), jnp.float32),
+        grid=(groups,),
+        out_shape=jax.ShapeDtypeStruct((vecs, vecs), F32),
         in_specs=[smem, smem, smem, smem,
-                  pl.BlockSpec((GROUP, 2, cycles, samples), lambda g: (g, 0, 0, 0)),
-                  pl.BlockSpec(memory_space=pltpu.VMEM)],
+                  pl.BlockSpec(block, lambda g: (jnp.minimum(g + 1, groups - 1), 0, 0, 0)),
+                  pl.BlockSpec(block, lambda g: (0, 0, 0, 0), pipeline_mode=pl.Buffered(1)),
+                  pl.BlockSpec(bg.shape, lambda g: (0, 0, 0, 0), pipeline_mode=pl.Buffered(1))],
         out_specs=pl.BlockSpec((vecs, vecs), lambda g: (0, 0)),
         scratch_shapes=[
-            pltpu.VMEM((256, 256), jnp.bfloat16),
-            pltpu.VMEM((2, 4, cycles, 8, samples), jnp.float32),
-            pltpu.VMEM((2, cycles, GROUP, samples), jnp.float32),
-            pltpu.VMEM((2, cycles, GROUP, samples), jnp.float32),
-            pltpu.VMEM((2, cycles, vecs, samples), jnp.bfloat16),
-            pltpu.VMEM((2, cycles, vecs, samples), jnp.bfloat16),
-            pltpu.VMEM((vecs, vecs), jnp.float32),
+            pltpu.VMEM((256, 256), BF16),
+            pltpu.VMEM((256, 256), BF16),
+            pltpu.VMEM((2, 4, cycles, 8, samples), F32),
+            pltpu.VMEM((2, cycles, GROUP, samples), F32),
+            pltpu.VMEM((2, cycles, GROUP, samples), F32),
+            pltpu.VMEM((2, cycles, vecs, samples), BF16),
+            pltpu.VMEM((2, cycles, vecs, samples), BF16),
+            pltpu.VMEM((2, 2, 8, 128, 256), BF16),
+            pltpu.VMEM(bg.shape, F32),
+            pltpu.VMEM((vecs, vecs), F32),
         ],
-        compiler_params=pltpu.CompilerParams(vmem_limit_bytes=60 * 1024 * 1024),
+        compiler_params=pltpu.CompilerParams(vmem_limit_bytes=63 * 1024 * 1024),
         name="segment_transfer",
-    )(nbr, steps, det, disp, basis, bg)
+    )(nbr.T, steps, det, disp, basis, basis, bg)
 
 
 def split2(x):

time: 126 us -> 76.6 us (0.61)
  Pallas kernels: 121 us -> 72.1 us
  local copies, waits for them, and re-layouts: 4.31 us -> 2.95 us
    pallas_call x1, Pallas kernels: 94.4 us -> 39.7 us  [segment_transfer(): pl.pallas_call(_transfer_kernel, grid=(groups,), out_shape=jax.ShapeDtype...]
    pallas_call x1, Pallas kernels: 26.2 us -> 32.5 us  [chain(): pl.pallas_call(_chain_kernel, out_shape=(shape, shape), in_specs=[vm], ou...]
    unnamed x3 -> x2, local copies, waits for them, and re-layouts: 4.31 us -> 2.95 us
where the time goes in v4:
time: 76.6 us; the launch traced here: 76.4 us
  Pallas kernels  72.1 us (94%)
  local copies, waits for them, and re-layouts  2.95 us (4%)
  between operations  1.29 us (2%)
    pallas_call x1, Pallas kernels, segment_transfer(): pl.pallas_call(_transfer_kernel, grid=(groups,), out_shape=jax.ShapeDtype...  39.7 us
    pallas_call x1, Pallas kernels, chain(): pl.pallas_call(_chain_kernel, out_shape=(shape, shape), in_specs=[vm], ou...  32.5 us
    unnamed x2, local copies, waits for them, and re-layouts  2.95 us

profile of v4, /device:TPU:1, one launch (start us, length us, event | category | flops | bytes accessed | tf_op | source)
XLA Modules:
  0.0 76.4 jit_solution(1898293115311104917)
XLA Ops:
  1.3 39.7 %segment_transfer.1.t_ref = f32[128,128]{1,0:T(8,128)} custom-call(s32[2,32]{1,0:T(2,128)} %bitcast.7, s32[1]{0:T(128)} %bitcast.4.steps, f32[32]{0:T(128)} %det.1, f32[32]{0:T(128)} %disp.1, bf16[128,2,32,1024]{3,2,1,0:T(8,128)(2,1)} %first.1, bf16[128,2,32,1024]{3,2,1,0:T(8,128)(2,1)} %first.1, f32[2,2,32,1024]{3,2,1,0:T(8,128)} %bitcast.5), custom_call_target="tpu_custom_call" | custom-call | tf_op jit(solution)/shard_map/segment_transfer/pallas_call | solution.py:202
  40.9 32.5 %chain_products.1 = (f32[128,128]{1,0:T(8,128)}, f32[128,128]{1,0:T(8,128)}) custom-call(f32[128,128]{1,0:T(8,128)} %segment_transfer.1.t_ref), custom_call_target="tpu_custom_call" | custom-call | tf_op jit(solution)/shard_map/chain_products/pallas_call | solution.py:316
  73.4 1.5 %copy.11 = f32[1,1,128,128]{3,2,1,0:T(8,128)} copy(f32[1,1,128,128]{3,2,1,0:T(8,128)} %bitcast.6) | data formatting | bytes 131072
  74.9 1.5 %copy.12 = f32[128,128]{1,0:T(8,128)} copy(f32[128,128]{1,0:T(8,128)} %get-tuple-element.9) | data formatting | bytes 131072

commit v5 on v4

--- a/solution.py
+++ b/solution.py
@@ -7,7 +7,7 @@
 from jax.sharding import PartitionSpec as P
 
 GROUP = 16
-UNROLL = 16
+UNROLL = 32
 F32, BF16 = jnp.float32, jnp.bfloat16
 
 
@@ -43,24 +43,18 @@
     def turn(left, x):
         return lax.dot_general(left, x, (((1,), (1,)), ((), ())), preferred_element_type=F32)
 
-    def mix_columns(src, ii):
-      for i in (2 * ii, 2 * ii + 1):
-        cols = pl.ds(pl.multiple_of(i * 256, 256), 256)
-        dest = pl.ds(pl.multiple_of(i * 32, 32), 32)
-        for p in range(2):
-            for h in range(2):
-                y = turn(colp[...], src[:, p, h * 16:(h + 1) * 16, cols].reshape(256, 256))
-                mixed[p, h, :, dest, :] = y.astype(BF16).reshape(8, 32, 256)
-
-    def swap_rows(ii, group):
-      for i in (2 * ii, 2 * ii + 1):
-        cols = pl.ds(pl.multiple_of(i * 256, 256), 256)
+    def mix_tile(src, k):
+        p, h, n = k // 8, k // 4 % 2, k % 4
+        y = turn(colp[...], src[:, p, h * 16:(h + 1) * 16, n * 256:(n + 1) * 256].reshape(256, 256))
+        mixed[p, h, :, n * 32:(n + 1) * 32, :] = y.astype(BF16).reshape(8, 32, 256)
+
+    def swap_tile(group, k):
+        p, h, n = k // 8, k // 4 % 2, k % 4
         dest = pl.ds(pl.multiple_of(group * GROUP, GROUP), GROUP)
-        for p in range(2):
-            for h in range(2):
-                y = turn(rowp[...], mixed[p, h, pl.ds(2 * i, 2)].reshape(256, 256)).reshape(16, 16, 256)
-                w0[p, h * 16:(h + 1) * 16, :, cols] = y
-                bc[p, h * 16:(h + 1) * 16, dest, cols] = y.astype(BF16)
+        cols = slice(n * 256, (n + 1) * 256)
+        y = turn(rowp[...], mixed[p, h, 2 * n:2 * n + 2].reshape(256, 256)).reshape(16, 16, 256)
+        w0[p, h * 16:(h + 1) * 16, :, cols] = y
+        bc[p, h * 16:(h + 1) * 16, dest, cols] = y.astype(BF16)
 
     @pl.when(g == 0)
     def _():
@@ -84,25 +78,22 @@
             x = jnp.concatenate([mixed[k // 2, k % 2, n, :, 0:lines] for k in range(3)], axis=1)
             bgp[:, :, :, n * 128:(n + 1) * 128] = turn(same, x).reshape(2, 2, cycles, 128)
 
-        @pl.loop(0, cycles)
-        def _(r):
-            for t in range(2):
+        @pl.loop(0, cycles // 4)
+        def _(q):
+          for r, t in [(4 * q + k, t) for k in range(4) for t in range(2)]:
                 a = bgp[t, 0, pl.ds(r, 1), :]
                 b = bgp[t, 1, pl.ds(r, 1), :]
                 inten = 2.0 * (a * a + b * b)
                 p = a * a - b * b
-                q = 2.0 * a * b
+                ab = 2.0 * a * b
                 lin = (det[r] + 2.0 * disp[r]) - inten
-                for k, val in enumerate((9.0 - q, lin + p, 9.0 + q, p - lin)):
+                for k, val in enumerate((9.0 - ab, lin + p, 9.0 + ab, p - lin)):
                     co[t, k, r] = jnp.broadcast_to(val, (8, samples))
 
-        @pl.loop(0, parts)
-        def _(i):
-            mix_columns(first, i)
-
-        @pl.loop(0, parts)
-        def _(i):
-            swap_rows(i, 0)
+        for k in range(16):
+            mix_tile(first, k)
+        for k in range(16):
+            swap_tile(0, k)
 
     def around(x):
         col = [x[:, 128 * k:128 * k + 128] for k in range(8)]
@@ -129,36 +120,33 @@
                 res[1][h].append((c2 * v + c3 * u) + (beta * au[h][:, lane] + cu))
         return [[jnp.concatenate(x, axis=1) for x in p] for p in res]
 
-    @pl.loop(0, parts)
-    def _(i):
-        mix_columns(basis, i)
-        for r in [i * UNROLL + k for k in range(UNROLL)]:
-            new = advance(w0, 0, r)
+    for r in range(cycles):
+        new = advance(w0, 0, r)
+        if r % 2 == 0:
+            mix_tile(basis, r // 2)
+        for p in range(2):
+            for h in range(2):
+                w1[p, r, 8 * h:8 * h + 8, :] = new[p][h]
+
+    rows = pl.ds(pl.multiple_of(g * GROUP, GROUP), GROUP)
+
+    @pl.when(steps[0] >= 2)
+    def _():
+        for r in range(cycles):
+            if r % 2 == 0:
+                swap_tile(later, r // 2)
+            new = advance(w1, 1, r)
             for p in range(2):
-                for h in range(2):
-                    w1[p, r, 8 * h:8 * h + 8, :] = new[p][h]
-
-    rows = pl.ds(pl.multiple_of(g * GROUP, GROUP), GROUP)
-
-    @pl.when(steps[0] >= 2)
-    def _():
-        @pl.loop(0, parts)
-        def _(i):
-            swap_rows(i, later)
-            for r in [i * UNROLL + k for k in range(UNROLL)]:
-                new = advance(w1, 1, r)
-                for p in range(2):
-                    full = jnp.concatenate([0.01 * x for x in new[p]], axis=0)
-                    pr[p, r, rows, :] = full.astype(BF16)
+                full = jnp.concatenate([0.01 * x for x in new[p]], axis=0)
+                pr[p, r, rows, :] = full.astype(BF16)
 
     @pl.when(steps[0] < 2)
     def _():
-        @pl.loop(0, parts)
-        def _(i):
-            swap_rows(i, later)
-            for r in [i * UNROLL + k for k in range(UNROLL)]:
-                for p in range(2):
-                    pr[p, r, rows, :] = (0.1 * w1[p, r]).astype(BF16)
+        for r in range(cycles):
+            if r % 2 == 0:
+                swap_tile(later, r // 2)
+            for p in range(2):
+                pr[p, r, rows, :] = (0.1 * w1[p, r]).astype(BF16)
 
     @pl.when(g == last)
     def _():
@@ -237,7 +225,7 @@
                    preferred_element_type=jnp.float32)
 
 
-def _chain_kernel(t_ref, pre_ref, mono_ref, slots, pair, low, before, send_sem, recv_sem):
+def _chain_kernel(t_ref, ends, slots, pair, low, before, send_sem, recv_sem):
     seq, grp = lax.axis_index("seq"), lax.axis_index("grp")
     core = lax.rem(grp, 2)
     depth = lax.rem(lax.div(grp, 2), 4)
@@ -255,7 +243,7 @@
             pl.semaphore_signal(barrier, inc=1, device_id=place(lax.rem(pos + hop, radix)), device_id_type=mesh_id)
     pl.semaphore_wait(barrier, sum(r[0] - 1 for r in rounds))
 
-    def prefix_step(k, last):
+    def prefix_step(k):
         radix, pos, _ = rounds[k]
 
         @pl.when(pos == 1)
@@ -275,7 +263,8 @@
     n = t_ref.shape[0]
     i = lax.broadcasted_iota(jnp.int32, (n, n), 0)
     j = lax.broadcasted_iota(jnp.int32, (n, n), 1)
-    before[...] = jnp.where(i == j, 1.0, 0.0)
+    eye = jnp.where(i == j, 1.0, 0.0)
+    before[...] = eye
     sends = []
     own = t_ref
     for k, (radix, pos, place) in enumerate(rounds):
@@ -289,37 +278,60 @@
         sends += copies
         slots[k, pos] = own[...]
         if k:
-            prefix_step(k - 1, False)
+            prefix_step(k - 1)
         for copy in copies:
             copy.wait_recv()
+        if k + 1 == len(rounds):
+            break
+        total = mm3(slots[k, 1], slots[k, 0])
         if radix == 4:
-            first = mm3(slots[k, 1], slots[k, 0])
-            low[...] = first
-            total = mm3(mm3(slots[k, 3], slots[k, 2]), first)
-        else:
-            total = mm3(slots[k, 1], slots[k, 0])
-        if k + 1 < len(rounds):
-            pair[k] = total
-            own = pair.at[k]
-        else:
-            mono_ref[...] = total
-    prefix_step(len(rounds) - 1, True)
-    pre_ref[...] = before[...]
+            low[...] = total
+            total = mm3(mm3(slots[k, 3], slots[k, 2]), total)
+        pair[k] = total
+        own = pair.at[k]
+
+    k = len(rounds) - 1
+    first = mm3(slots[k, 1], slots[k, 0])
+    ends[0] = mm3(slots[k, 3], slots[k, 2])
+    ends[1] = first
+    ends[2] = before[...]
+    ends[3] = first
+
+    @pl.when(wide == 3)
+    def _():
+        ends[2] = mm3(before[...], slots[k, 2])
+
+    @pl.when(wide == 1)
+    def _():
+        ends[3] = slots[k, 0]
+
+    @pl.when(wide == 0)
+    def _():
+        ends[3] = eye
+
     for copy in sends:
         copy.wait_send()
+
+
+def _finish_kernel(ends, pre_ref, mono_ref):
+    mono_ref[...] = mm3(ends[0], ends[1])
+    pre_ref[...] = mm3(ends[2], ends[3])
 
 
 def chain(t):
     n = t.shape[0]
     shape = jax.ShapeDtypeStruct((n, n), jnp.float32)
     vm = pl.BlockSpec(memory_space=pltpu.VMEM)
-    return pl.pallas_call(
-        _chain_kernel, out_shape=(shape, shape), in_specs=[vm], out_specs=(vm, vm),
+    ends = pl.pallas_call(
+        _chain_kernel, out_shape=jax.ShapeDtypeStruct((4, n, n), jnp.float32), in_specs=[vm], out_specs=vm,
         scratch_shapes=[pltpu.VMEM((4, 4, n, n), jnp.float32), pltpu.VMEM((3, n, n), jnp.float32),
                         pltpu.VMEM((n, n), jnp.float32), pltpu.VMEM((n, n), jnp.float32),
                         pltpu.SemaphoreType.DMA((4, 4)), pltpu.SemaphoreType.DMA((4, 4))],
         compiler_params=pltpu.CompilerParams(collective_id=0, has_side_effects=True),
         name="chain_products")(t)
+    return pl.pallas_call(
+        _finish_kernel, out_shape=(shape, shape), in_specs=[vm], out_specs=(vm, vm),
+        name="last_products")(ends)
 
 def shards(basis, background, detuning, dispersion, neighbors, step_counts):
     own = segment_transfer(

time: 76.6 us -> 73.3 us (0.957)
  local copies, waits for them, and re-layouts: 2.95 us -> 0 us
    pallas_call x1, Pallas kernels: 39.7 us -> 34.8 us  [segment_transfer(): pl.pallas_call(_transfer_kernel, grid=(groups,), out_shape=jax.ShapeDtype...]
    pallas_call x1 -> x2, Pallas kernels: 32.5 us -> 37 us  [the longest x1 35.3 us: chain(): pl.pallas_call(_chain_kernel, out_shape=jax.ShapeDtypeStruct((4, n, n), j...]
    unnamed x2 -> x0, local copies, waits for them, and re-layouts: 2.95 us -> none
where the time goes in v5:
time: 73.3 us; the launch traced here: 73.1 us
  Pallas kernels  71.8 us (98%)
  between operations  1.29 us (2%)
    pallas_call x1, Pallas kernels, chain(): pl.pallas_call(_chain_kernel, out_shape=jax.ShapeDtypeStruct((4, n, n), j...  35.3 us
    pallas_call x1, Pallas kernels, segment_transfer(): pl.pallas_call(_transfer_kernel, grid=(groups,), out_shape=jax.ShapeDtype...  34.8 us
    pallas_call x1, Pallas kernels, chain(): pl.pallas_call(_finish_kernel, out_shape=(shape, shape), in_specs=[vm], o...  1.79 us

profile of v5, /device:TPU:1, one launch (start us, length us, event | category | flops | bytes accessed | tf_op | source)
XLA Modules:
  0.0 73.1 jit_solution(17113593720490496487)
XLA Ops:
  1.3 34.8 %segment_transfer.1.t_ref = f32[128,128]{1,0:T(8,128)} custom-call(s32[2,32]{1,0:T(2,128)} %bitcast.6, s32[1]{0:T(128)} %bitcast.4.steps, f32[32]{0:T(128)} %det.1, f32[32]{0:T(128)} %disp.1, bf16[128,2,32,1024]{3,2,1,0:T(8,128)(2,1)} %first.1, bf16[128,2,32,1024]{3,2,1,0:T(8,128)(2,1)} %first.1, f32[2,2,32,1024]{3,2,1,0:T(8,128)} %bitcast.5), custom_call_target="tpu_custom_call" | custom-call | tf_op jit(solution)/shard_map/segment_transfer/pallas_call | solution.py:190
  36.0 35.3 %chain_products.1.ends = f32[4,128,128]{2,1,0:T(8,128)} custom-call(f32[128,128]{1,0:T(8,128)} %segment_transfer.1.t_ref), custom_call_target="tpu_custom_call" | custom-call | tf_op jit(solution)/shard_map/chain_products/pallas_call | solution.py:325
  71.3 1.8 %last_products.1 = (f32[128,128]{1,0:T(8,128)}, f32[128,128]{1,0:T(8,128)}) custom-call(f32[4,128,128]{2,1,0:T(8,128)} %chain_products.1.ends), custom_call_target="tpu_custom_call" | custom-call | tf_op jit(solution)/shard_map/last_products/pallas_call | solution.py:332

commit v6 on v5

--- a/solution.py
+++ b/solution.py
@@ -33,19 +33,23 @@
     return jnp.dot(left6(a), right6(b), preferred_element_type=F32)
 
 
-def _transfer_kernel(nbr, steps, det, disp, basis, first, bg, out, rowp, colp, co, w0, w1, bc, pr, mixed, bgp, acc):
+def _transfer_kernel(nbr, steps, det, disp, basis, bg, out, rowp, colp, co, w0, w1, bc, pr, mixed, bgp, acc, stage, sems):
     g = pl.program_id(0)
     last = pl.num_programs(0) - 1
     vecs, cycles, samples = bc.shape[2], bc.shape[1], bc.shape[3]
     parts = cycles // UNROLL
-    later = jnp.minimum(g + 1, last)
+    later = g + 1
+    slot = lax.rem(later, 2)
+
+    def fetch(block, where):
+        return pltpu.make_async_copy(basis.at[pl.ds(block * GROUP, GROUP)], stage.at[where], sems.at[where])
 
     def turn(left, x):
         return lax.dot_general(left, x, (((1,), (1,)), ((), ())), preferred_element_type=F32)
 
-    def mix_tile(src, k):
+    def mix_tile(where, k):
         p, h, n = k // 8, k // 4 % 2, k % 4
-        y = turn(colp[...], src[:, p, h * 16:(h + 1) * 16, n * 256:(n + 1) * 256].reshape(256, 256))
+        y = turn(colp[...], stage[where, :, p, h * 16:(h + 1) * 16, n * 256:(n + 1) * 256].reshape(256, 256))
         mixed[p, h, :, n * 32:(n + 1) * 32, :] = y.astype(BF16).reshape(8, 32, 256)
 
     def swap_tile(group, k):
@@ -58,6 +62,8 @@
 
     @pl.when(g == 0)
     def _():
+        fetch(0, 0).start()
+        fetch(1, 1).start()
         i = lax.broadcasted_iota(jnp.int32, (256, 256), 0)
         j = lax.broadcasted_iota(jnp.int32, (256, 256), 1)
         hit = jnp.logical_and(i // 16 == j % 16, i % 16 == j // 16)
@@ -90,8 +96,10 @@
                 for k, val in enumerate((9.0 - ab, lin + p, 9.0 + ab, p - lin)):
                     co[t, k, r] = jnp.broadcast_to(val, (8, samples))
 
+        fetch(0, 0).wait()
         for k in range(16):
-            mix_tile(first, k)
+            mix_tile(0, k)
+        fetch(2, 0).start()
         for k in range(16):
             swap_tile(0, k)
 
@@ -120,33 +128,52 @@
                 res[1][h].append((c2 * v + c3 * u) + (beta * au[h][:, lane] + cu))
         return [[jnp.concatenate(x, axis=1) for x in p] for p in res]
 
-    for r in range(cycles):
-        new = advance(w0, 0, r)
-        if r % 2 == 0:
-            mix_tile(basis, r // 2)
-        for p in range(2):
-            for h in range(2):
-                w1[p, r, 8 * h:8 * h + 8, :] = new[p][h]
-
     rows = pl.ds(pl.multiple_of(g * GROUP, GROUP), GROUP)
 
-    @pl.when(steps[0] >= 2)
-    def _():
+    def first_step(more):
         for r in range(cycles):
-            if r % 2 == 0:
+            new = advance(w0, 0, r)
+            if more and r % 2 == 0:
+                mix_tile(slot, r // 2)
+            for p in range(2):
+                for h in range(2):
+                    w1[p, r, 8 * h:8 * h + 8, :] = new[p][h]
+
+    def second_step(more):
+        for r in range(cycles):
+            if more and r % 2 == 0:
                 swap_tile(later, r // 2)
             new = advance(w1, 1, r)
             for p in range(2):
                 full = jnp.concatenate([0.01 * x for x in new[p]], axis=0)
                 pr[p, r, rows, :] = full.astype(BF16)
 
-    @pl.when(steps[0] < 2)
-    def _():
+    def keep_first(more):
         for r in range(cycles):
-            if r % 2 == 0:
+            if more and r % 2 == 0:
                 swap_tile(later, r // 2)
             for p in range(2):
                 pr[p, r, rows, :] = (0.1 * w1[p, r]).astype(BF16)
+
+    twice = steps[0] >= 2
+
+    @pl.when(g < last)
+    def _():
+        fetch(later, slot).wait()
+        first_step(True)
+
+        @pl.when(g + 3 <= last)
+        def _():
+            fetch(g + 3, slot).start()
+
+        pl.when(twice)(functools.partial(second_step, True))
+        pl.when(jnp.logical_not(twice))(functools.partial(keep_first, True))
+
+    @pl.when(g == last)
+    def _():
+        first_step(False)
+        pl.when(twice)(functools.partial(second_step, False))
+        pl.when(jnp.logical_not(twice))(functools.partial(keep_first, False))
 
     @pl.when(g == last)
     def _():
@@ -192,8 +219,7 @@
         grid=(groups,),
         out_shape=jax.ShapeDtypeStruct((vecs, vecs), F32),
         in_specs=[smem, smem, smem, smem,
-                  pl.BlockSpec(block, lambda g: (jnp.minimum(g + 1, groups - 1), 0, 0, 0)),
-                  pl.BlockSpec(block, lambda g: (0, 0, 0, 0), pipeline_mode=pl.Buffered(1)),
+                  pl.BlockSpec(memory_space=pl.ANY),
                   pl.BlockSpec(bg.shape, lambda g: (0, 0, 0, 0), pipeline_mode=pl.Buffered(1))],
         out_specs=pl.BlockSpec((vecs, vecs), lambda g: (0, 0)),
         scratch_shapes=[
@@ -207,10 +233,12 @@
             pltpu.VMEM((2, 2, 8, 128, 256), BF16),
             pltpu.VMEM(bg.shape, F32),
             pltpu.VMEM((vecs, vecs), F32),
+            pltpu.VMEM((2,) + block, BF16),
+            pltpu.SemaphoreType.DMA((2,)),
         ],
         compiler_params=pltpu.CompilerParams(vmem_limit_bytes=63 * 1024 * 1024),
         name="segment_transfer",
-    )(nbr.T, steps, det, disp, basis, basis, bg)
+    )(nbr.T, steps, det, disp, basis, bg)
 
 
 def split2(x):
@@ -269,7 +297,7 @@
     own = t_ref
     for k, (radix, pos, place) in enumerate(rounds):
         copies = []
-        for hop in ((2, 1, 3) if radix == 4 else (1,)):
+        for hop in ((1, 3, 2) if radix == 4 else (1,)):
             copy = pltpu.make_async_remote_copy(
                 src_ref=own, dst_ref=slots.at[k, pos], send_sem=send_sem.at[k, hop], recv_sem=recv_sem.at[k, hop],
                 device_id=place(lax.rem(pos + hop, radix)), device_id_type=mesh_id)

time: 73.3 us -> 70.8 us (0.966)
  Pallas kernels: 71.8 us -> 69.4 us
    pallas_call x1, Pallas kernels: 34.8 us -> 32.5 us  [segment_transfer(): pl.pallas_call(_transfer_kernel, grid=(groups,), out_shape=jax.ShapeDtype...]
where the time goes in v6:
time: 70.8 us; the launch traced here: 70.7 us
  Pallas kernels  69.4 us (98%)
  between operations  1.29 us (2%)
    pallas_call x1, Pallas kernels, chain(): pl.pallas_call(_chain_kernel, out_shape=jax.ShapeDtypeStruct((4, n, n), j...  35.1 us
    pallas_call x1, Pallas kernels, segment_transfer(): pl.pallas_call(_transfer_kernel, grid=(groups,), out_shape=jax.ShapeDtype...  32.5 us
    pallas_call x1, Pallas kernels, chain(): pl.pallas_call(_finish_kernel, out_shape=(shape, shape), in_specs=[vm], o...  1.78 us

profile of v6, /device:TPU:1, one launch (start us, length us, event | category | flops | bytes accessed | tf_op | source)
XLA Modules:
  0.0 70.7 jit_solution(17162960052035658741)
XLA Ops:
  1.3 32.5 %segment_transfer.1.t_ref = f32[128,128]{1,0:T(8,128)} custom-call(s32[2,32]{1,0:T(2,128)} %bitcast.6, s32[1]{0:T(128)} %bitcast.4.steps, f32[32]{0:T(128)} %det.1, f32[32]{0:T(128)} %disp.1, bf16[128,2,32,1024]{3,2,1,0:T(8,128)(2,1)} %basis.1, f32[2,2,32,1024]{3,2,1,0:T(8,128)} %bitcast.5), custom_call_target="tpu_custom_call" | custom-call | tf_op jit(solution)/shard_map/segment_transfer/pallas_call | solution.py:217
  33.8 35.1 %chain_products.1.ends = f32[4,128,128]{2,1,0:T(8,128)} custom-call(f32[128,128]{1,0:T(8,128)} %segment_transfer.1.t_ref), custom_call_target="tpu_custom_call" | custom-call | tf_op jit(solution)/shard_map/chain_products/pallas_call | solution.py:353
  68.9 1.8 %last_products.1 = (f32[128,128]{1,0:T(8,128)}, f32[128,128]{1,0:T(8,128)}) custom-call(f32[4,128,128]{2,1,0:T(8,128)} %chain_products.1.ends), custom_call_target="tpu_custom_call" | custom-call | tf_op jit(solution)/shard_map/last_products/pallas_call | solution.py:360

commit v7 on v6

--- a/solution.py
+++ b/solution.py
@@ -200,13 +200,13 @@
         prod = scale * (eye + 2.0 * gen - gram)
 
         def more(c):
-            return c[0] > 1e-7
+            return 1.0 - c[0] > 3e-7
 
         def body(c):
-            rho, rs, pd = c
-            return rho * rho, mm(rs, rs), pd + mm(rs, pd)
-
-        out[...] = lax.while_loop(more, body, (0.5 * bound * scale, resid, prod))[2]
+            gap, rs, pd = c
+            return gap * (2.0 - gap), mm(rs, rs), pd + mm(rs, pd)
+
+        out[...] = lax.while_loop(more, body, (scale, resid, prod))[2]
 
 
 def segment_transfer(basis, bg, det, disp, nbr, steps):

time: 70.8 us -> 71.1 us (level)
  no operation moved by 1% of the time
where the time goes in v7:
time: 71.1 us; the launch traced here: 70.9 us
  Pallas kernels  69.6 us (98%)
  between operations  1.29 us (2%)
    pallas_call x1, Pallas kernels, chain(): pl.pallas_call(_chain_kernel, out_shape=jax.ShapeDtypeStruct((4, n, n), j...  35.4 us
    pallas_call x1, Pallas kernels, segment_transfer(): pl.pallas_call(_transfer_kernel, grid=(groups,), out_shape=jax.ShapeDtype...  32.5 us
    pallas_call x1, Pallas kernels, chain(): pl.pallas_call(_finish_kernel, out_shape=(shape, shape), in_specs=[vm], o...  1.79 us

profile of v7, /device:TPU:1, one launch (start us, length us, event | category | flops | bytes accessed | tf_op | source)
XLA Modules:
  0.0 70.9 jit_solution(8272340370137823359)
XLA Ops:
  1.3 32.5 %segment_transfer.1.t_ref = f32[128,128]{1,0:T(8,128)} custom-call(s32[2,32]{1,0:T(2,128)} %bitcast.6, s32[1]{0:T(128)} %bitcast.4.steps, f32[32]{0:T(128)} %det.1, f32[32]{0:T(128)} %disp.1, bf16[128,2,32,1024]{3,2,1,0:T(8,128)(2,1)} %basis.1, f32[2,2,32,1024]{3,2,1,0:T(8,128)} %bitcast.5), custom_call_target="tpu_custom_call" | custom-call | tf_op jit(solution)/shard_map/segment_transfer/pallas_call | solution.py:217
  33.8 35.4 %chain_products.1.ends = f32[4,128,128]{2,1,0:T(8,128)} custom-call(f32[128,128]{1,0:T(8,128)} %segment_transfer.1.t_ref), custom_call_target="tpu_custom_call" | custom-call | tf_op jit(solution)/shard_map/chain_products/pallas_call | solution.py:353
  69.1 1.8 %last_products.1 = (f32[128,128]{1,0:T(8,128)}, f32[128,128]{1,0:T(8,128)}) custom-call(f32[4,128,128]{2,1,0:T(8,128)} %chain_products.1.ends), custom_call_target="tpu_custom_call" | custom-call | tf_op jit(solution)/shard_map/last_products/pallas_call | solution.py:360

commit v8 on v7

--- a/solution.py
+++ b/solution.py
@@ -204,7 +204,8 @@
 
         def body(c):
             gap, rs, pd = c
-            return gap * (2.0 - gap), mm(rs, rs), pd + mm(rs, pd)
+            both = jnp.dot(left6(rs), jnp.concatenate([right6(rs), right6(pd)], axis=1), preferred_element_type=F32)
+            return gap * (2.0 - gap), both[:, :vecs], pd + both[:, vecs:]
 
         out[...] = lax.while_loop(more, body, (scale, resid, prod))[2]
 

time: 71.1 us -> 70.2 us (0.987)
  Pallas kernels: 69.6 us -> 68.7 us
where the time goes in v8:
time: 70.2 us; the launch traced here: 70 us
  Pallas kernels  68.7 us (98%)
  between operations  1.29 us (2%)
    pallas_call x1, Pallas kernels, chain(): pl.pallas_call(_chain_kernel, out_shape=jax.ShapeDtypeStruct((4, n, n), j...  34.7 us
    pallas_call x1, Pallas kernels, segment_transfer(): pl.pallas_call(_transfer_kernel, grid=(groups,), out_shape=jax.ShapeDtype...  32.2 us
    pallas_call x1, Pallas kernels, chain(): pl.pallas_call(_finish_kernel, out_shape=(shape, shape), in_specs=[vm], o...  1.79 us

profile of v8, /device:TPU:1, one launch (start us, length us, event | category | flops | bytes accessed | tf_op | source)
XLA Modules:
  0.0 70.0 jit_solution(7450015066072105313)
XLA Ops:
  1.3 32.2 %segment_transfer.1.t_ref = f32[128,128]{1,0:T(8,128)} custom-call(s32[2,32]{1,0:T(2,128)} %bitcast.6, s32[1]{0:T(128)} %bitcast.4.steps, f32[32]{0:T(128)} %det.1, f32[32]{0:T(128)} %disp.1, bf16[128,2,32,1024]{3,2,1,0:T(8,128)(2,1)} %basis.1, f32[2,2,32,1024]{3,2,1,0:T(8,128)} %bitcast.5), custom_call_target="tpu_custom_call" | custom-call | tf_op jit(solution)/shard_map/segment_transfer/pallas_call | solution.py:218
  33.5 34.7 %chain_products.1.ends = f32[4,128,128]{2,1,0:T(8,128)} custom-call(f32[128,128]{1,0:T(8,128)} %segment_transfer.1.t_ref), custom_call_target="tpu_custom_call" | custom-call | tf_op jit(solution)/shard_map/chain_products/pallas_call | solution.py:354
  68.2 1.8 %last_products.1 = (f32[128,128]{1,0:T(8,128)}, f32[128,128]{1,0:T(8,128)}) custom-call(f32[4,128,128]{2,1,0:T(8,128)} %chain_products.1.ends), custom_call_target="tpu_custom_call" | custom-call | tf_op jit(solution)/shard_map/last_products/pallas_call | solution.py:361
